TPU v7x, 256 devices: a whole 4x4x8 slice. The times are simulated.
256 devices in a mesh: lat: 8 (over y, x_lo), lon: 32 (over x_hi, z, core).
Axes of the slice: x: 4 (x_hi: 2, x_lo: 2; x = x_hi * 2 + x_lo), y: 4, z: 8, core: 2. Of those that a mesh axis runs over, the one named last changes fastest.
Arguments:
- tokens_in: bfloat16 [2, 96, 768, 1024], P(None, 'lat', 'lon'), may hold values from -6 to 6
- grad_out: bfloat16 [2, 96, 768, 1024], P(None, 'lat', 'lon'), may hold values from -6 to 6
- norm_gain: float32 [1024], replicated, may hold values from 0.25 to 1.75
- w_qkv: bfloat16 [1024, 1536], replicated
- w_proj: bfloat16 [512, 1024], replicated, may hold values from -0.25 to 0.25
Outputs:
- grad_in: bfloat16 [2, 96, 768, 1024], P(None, 'lat', 'lon')
- grad_qkv: float32 [1024, 1536], P(('lat', 'lon'))
- grad_proj: float32 [512, 1024], P(None, ('lat', 'lon'))
- gain_gradient: float32 [1024], P(('lat', 'lon'))
All inputs are finite; a program needn't handle non-finite values.
Results may differ from a plain program's by a relative error of at most 0.0095.
Values may be sent and summed in bfloat16 or wider, within the bound.
No kernel may reach another device: no remote copies, remote signals or barrier semaphores. Data moves between devices by JAX's collectives and lax.ppermute only.
A program may use at most 128 MiB of HBM per device.

v0:
```python
import functools

import jax
import jax.numpy as jnp
from jax import lax
from jax.experimental import pallas as pl
from jax.experimental.pallas import tpu as pltpu
from jax.sharding import Mesh, PartitionSpec as P


F32 = jnp.float32
BF = jnp.bfloat16
D = 1024
HH = 512
TOK = 144
NWIN = 4
ROWS = NWIN * TOK
LEV, NR, NC = 2, 12, 24
LATN = 112
LONN = 112
DIAGN = 48
EPS = 1e-05
FACTOR = 1.0 / 384.0

NN = (((1,), (0,)), ((), ()))
NT = (((1,), (1,)), ((), ()))
TN = (((0,), (0,)), ((), ()))


def dot(a, b, dims):
    return lax.dot_general(a, b, dims, preferred_element_type=F32)


def params(mib):
    return pltpu.CompilerParams(vmem_limit_bytes=mib * 1024 * 1024)


def cost(flops, nbytes):
    return pl.CostEstimate(flops=int(flops), bytes_accessed=int(nbytes), transcendentals=0)


def window_row(lev, rr, cc):
    return ((rr // 6) * 2 + cc // 12) * TOK + lev * 72 + (rr % 6) * 12 + cc % 12


def own_segments():
    for lev in range(LEV):
        for rr in range(9):
            base = (lev * NR + rr + 3) * NC
            yield base + 6, window_row(lev, rr, 0), 12
            yield base + 18, window_row(lev, rr, 12), 6


def lat_segments():
    for lev in range(LEV):
        for r in range(3):
            base = (lev * 3 + r) * 18
            yield base, window_row(lev, 9 + r, 0), 12, (lev * NR + r) * NC + 6
            yield base + 12, window_row(lev, 9 + r, 12), 6, (lev * NR + r) * NC + 18


def lon_segments():
    for lev in range(LEV):
        for rr in range(9):
            yield (lev * 9 + rr) * 6, window_row(lev, rr, 18), 6, (lev * NR + rr + 3) * NC


def diag_segments():
    for lev in range(LEV):
        for r in range(3):
            yield (lev * 3 + r) * 6, window_row(lev, 9 + r, 18), 6, (lev * NR + r) * NC


def pack_kernel(x_ref, dy_ref, lat_ref, lon_ref, diag_ref, top, side, src, dst, sems):
    copies = []
    for a, ref in enumerate((x_ref, dy_ref)):
        copies.append(
            (
                pltpu.make_async_copy(ref.at[:, 0:3], top.at[a], sems.at[a, 0]),
                pltpu.make_async_copy(ref.at[:, 3:12, 0:8, :], side.at[a], sems.at[a, 1]),
            )
        )
    for pair in copies:
        for copy in pair:
            copy.start()
    for a, pair in enumerate(copies):
        pair[0].wait()
        for lev in range(LEV):
            for r in range(3):
                at = (lev * NR + r) * NC
                src[at : at + NC, :] = top[a, lev, r].astype(F32)
        pair[1].wait()
        for lev in range(LEV):
            for r in range(3, NR):
                at = (lev * NR + r) * NC
                src[at : at + 8, :] = side[a, lev, r - 3].astype(F32)
        for out, segments in ((lat_ref, lat_segments), (lon_ref, lon_segments), (diag_ref, diag_segments)):
            count = out.shape[1]
            dst[count - 16 : count, :] = jnp.zeros((16, D), F32)
            for at, _, size, own in segments():
                dst[at : at + size, :] = src[own : own + size, :]
            out[a] = dst[:count, :].astype(BF)


def pack(x, dy):
    return pl.pallas_call(
        pack_kernel,
        in_specs=[pl.BlockSpec(memory_space=pltpu.HBM)] * 2,
        out_shape=(
            jax.ShapeDtypeStruct((2, LATN, D), BF),
            jax.ShapeDtypeStruct((2, LONN, D), BF),
            jax.ShapeDtypeStruct((2, DIAGN, D), BF),
        ),
        scratch_shapes=[
            pltpu.VMEM((2, LEV, 3, NC, D), BF),
            pltpu.VMEM((2, LEV, 9, 8, D), BF),
            pltpu.VMEM((ROWS, D), F32),
            pltpu.VMEM((LATN, D), F32),
            pltpu.SemaphoreType.DMA((2, 2)),
        ],
        compiler_params=params(60),
        cost_estimate=cost(1e6, 4e6),
        name="pack",
    )(x, dy)


def slot(at):
    return at // TOK


def assemble(slots, ref, halos, src, win):
    for lev in range(LEV):
        for r in range(3, 9) if slots[0] < 2 else range(9, NR):
            at = (lev * NR + r) * NC
            src[at : at + NC, :] = ref[lev, r].astype(F32)
    for own, at, size in own_segments():
        if slot(at) in slots:
            win[at : at + size, :] = src[own : own + size, :]
    for halo, segments in halos:
        count = halo.shape[-2]
        src[:count, :] = halo[...].astype(F32)
        for here, at, size, _ in segments():
            if slot(at) in slots:
                win[at : at + size, :] = src[here : here + size, :]


def layer_stats(x):
    mean = jnp.mean(x, -1, keepdims=True)
    cen = x - mean
    inv = lax.rsqrt(jnp.mean(cen * cen, -1, keepdims=True) + EPS)
    return cen, inv


def normalize(slots, base, win, gain_ref, xw_ref, nrm):
    for w in slots:
        x = win[w * TOK : (w + 1) * TOK, :]
        rows = slice((w - base) * TOK, (w - base + 1) * TOK)
        xw_ref[rows, :] = x.astype(BF)
        cen, inv = layer_stats(x)
        nrm[rows, :] = (cen * inv * gain_ref[...]).astype(BF)


def project(rows, nrm, dyw_ref, wq_ref, wp_ref, qkv, gatt):
    for j in range(6):
        cols = slice(j * 256, (j + 1) * 256)
        qkv[rows, cols] = dot(nrm[rows, :], wq_ref[:, cols], NN).astype(BF)
    for j in range(2):
        cols = slice(j * 256, (j + 1) * 256)
        gatt[rows, cols] = dot(dyw_ref[rows, :], wp_ref[cols, :], NT).astype(BF)


def attend(slots, base, qkv, gatt, gact_ref):
    low = lax.broadcasted_iota(jnp.int32, (TOK, 128), 1) < 64
    keyg = (lax.broadcasted_iota(jnp.int32, (TOK, 2 * TOK), 0) // 12) % 6 < 3
    qryg = (lax.broadcasted_iota(jnp.int32, (TOK, 2 * TOK), 1) // 12) % 6 < 3
    last = jnp.logical_and(lax.axis_index("y") == 3, lax.axis_index("xl") == 1)
    apart = jnp.logical_and(keyg != qryg, last)

    def stacked(v):
        z = jnp.zeros_like(v)
        return jnp.concatenate([jnp.where(low, v, z), jnp.where(low, z, v)], axis=0)

    for w in slots:
        rows = slice((w - base) * TOK, (w - base + 1) * TOK)
        for hp in range(4):
            at = hp * 128
            q2 = stacked(qkv[rows, at : at + 128] * jnp.bfloat16(0.125))
            k = qkv[rows, HH + at : HH + at + 128]
            v = qkv[rows, 2 * HH + at : 2 * HH + at + 128]
            g2 = stacked(gatt[rows, at : at + 128])
            s = dot(k, q2, NT)
            if w >= 2:
                s = jnp.where(apart, -1000000000.0, s)
            e = jnp.exp(s - jnp.max(s, 0, keepdims=True))
            p = e * (1.0 / jnp.sum(e, 0, keepdims=True))
            pb = p.astype(BF)
            dp = dot(v, g2, NT)
            ds = (p * (dp - jnp.sum(p * dp, 0, keepdims=True))).astype(BF)
            o = dot(pb, v, TN)
            gact_ref[rows, 3 * HH + at : 3 * HH + at + 128] = jnp.where(low, o[:TOK], o[TOK:]).astype(BF)
            dq = dot(ds, k, TN)
            gact_ref[rows, at : at + 128] = (jnp.where(low, dq[:TOK], dq[TOK:]) * 0.125).astype(BF)
            gact_ref[rows, HH + at : HH + at + 128] = dot(ds, q2, NN).astype(BF)
            gact_ref[rows, 2 * HH + at : 2 * HH + at + 128] = dot(pb, g2, NN).astype(BF)


def early_kernel(w, x_ref, dy_ref, *refs):
    halo, refs = (refs[0], refs[1:]) if w else (None, refs)
    gain_ref, wq_ref, wp_ref, nrm_ref, xw_ref, dyw_ref, gact_ref, src, win, qkv, gatt = refs
    halos = [((halo.at[a], lon_segments),) if w else () for a in range(2)]
    assemble((w,), x_ref, halos[0], src, win)
    normalize((w,), w, win, gain_ref, xw_ref, nrm_ref)
    assemble((w,), dy_ref, halos[1], src, win)
    dyw_ref[...] = win[w * TOK : (w + 1) * TOK, :].astype(BF)
    project(slice(0, TOK), nrm_ref, dyw_ref, wq_ref, wp_ref, qkv, gatt)
    attend((w,), w, qkv, gatt, gact_ref)


def early_call(w, *operands):
    wide = jax.ShapeDtypeStruct((TOK, D), BF)
    return pl.pallas_call(
        functools.partial(early_kernel, w),
        out_shape=(
            wide,
            wide,
            wide,
            jax.ShapeDtypeStruct((TOK, 2048), BF),
        ),
        scratch_shapes=[
            pltpu.VMEM((ROWS, D), F32),
            pltpu.VMEM((2 * TOK, D), F32),
            pltpu.VMEM((TOK, 1536), BF),
            pltpu.VMEM((TOK, HH), BF),
        ],
        compiler_params=params(16),
        cost_estimate=cost(2e9, 9e6),
    )(*operands)


def main_kernel(x_ref, dy_ref, lat_ref, lon_ref, diag_ref, gain_ref, wq_ref, wp_ref, *refs):
    early, refs = (refs[0:4], refs[4:8]), refs[8:]
    keep_ref, send_ref, gact_ref, xw_ref, dyw_ref, src, win, nrm, qkv, gatt, lhs = refs
    core = lax.axis_index("c")
    for w in range(2):
        for to, at in zip((nrm, xw_ref, dyw_ref, gact_ref), early[w]):
            to[w * TOK : (w + 1) * TOK, :] = at[...]
    rest = slice(2 * TOK, ROWS)
    for a, ref in enumerate((x_ref, dy_ref)):
        halos = ((lat_ref.at[a], lat_segments), (lon_ref.at[a], lon_segments), (diag_ref.at[a], diag_segments))
        assemble((2, 3), ref, halos, src, win)
        if a:
            dyw_ref[rest, :] = win[rest, :].astype(BF)
        else:
            normalize((2, 3), 0, win, gain_ref, xw_ref, nrm)
    project(rest, nrm, dyw_ref, wq_ref, wp_ref, qkv, gatt)
    attend((2, 3), 0, qkv, gatt, gact_ref)

    lhs[0] = nrm[...].T
    lhs[1] = dyw_ref[...].T
    for out, half in ((send_ref, 1 - core), (keep_ref, core)):
        low = pl.ds(pl.multiple_of(half * 1024, 1024), 512)
        high = pl.ds(pl.multiple_of(half * 1024 + 512, 512), 512)
        for i in range(4):
            rows = slice(i * 256, (i + 1) * 256)
            out[rows, 0:512] = dot(lhs[0, rows, :], gact_ref[:, low], NN).astype(BF)
            out[rows, 512:1024] = dot(lhs[half, rows, :], gact_ref[:, high], NN).astype(BF)


def main_call(*operands):
    return pl.pallas_call(
        main_kernel,
        out_shape=(
            jax.ShapeDtypeStruct((D, 1024), BF),
            jax.ShapeDtypeStruct((D, 1024), BF),
            jax.ShapeDtypeStruct((ROWS, 2048), BF),
            jax.ShapeDtypeStruct((ROWS, D), BF),
            jax.ShapeDtypeStruct((ROWS, D), BF),
        ),
        scratch_shapes=[
            pltpu.VMEM((ROWS, D), F32),
            pltpu.VMEM((ROWS, D), F32),
            pltpu.VMEM((ROWS, D), BF),
            pltpu.VMEM((ROWS, 1536), BF),
            pltpu.VMEM((ROWS, HH), BF),
            pltpu.VMEM((2, D, ROWS), BF),
        ],
        compiler_params=params(32),
        cost_estimate=cost(5.5e9, 14e6),
        name="main",
    )(*operands)


def input_rows(w, gact_ref, xw_ref, dyw_ref, gain, wq_ref, win):
    rows = slice(w * TOK, (w + 1) * TOK)
    gn = dot(gact_ref[rows, 0:1536], wq_ref[...], NT)
    cen, inv = layer_stats(xw_ref[rows, :].astype(F32))
    xhat = cen * inv
    g = gn * gain
    win[rows, :] = dyw_ref[rows, :].astype(F32) + inv * (
        g - jnp.mean(g, -1, keepdims=True) - xhat * jnp.mean(g * xhat, -1, keepdims=True)
    )
    return jnp.sum(gn * xhat, 0, keepdims=True)


def input_low_kernel(
    gact_ref, xw_ref, dyw_ref, gain_ref, wq_ref, own_ref, lat_ref, lon_ref, diag_ref, gg_ref, win, dst
):
    gain = gain_ref[...]
    gg_ref[...] = sum(input_rows(w, gact_ref, xw_ref, dyw_ref, gain, wq_ref, win) for w in (2, 3))
    for out, segments in ((lat_ref, lat_segments()), (lon_ref, lon_out_segments(0)), (diag_ref, diag_segments())):
        count = out.shape[0]
        dst[count - 16 : count, :] = jnp.zeros((16, D), F32)
        for at, here, size, _ in segments:
            dst[at : at + size, :] = win[here : here + size, :]
        out[...] = dst[:count, :].astype(BF)
    for own, here, size in own_segments():
        if slot(here) >= 2:
            dst[own : own + size, :] = win[here : here + size, :]
    for lev in range(LEV):
        for r in range(9, NR):
            at = (lev * NR + r) * NC
            own_ref[lev, r - 9] = dst[at : at + NC, :].astype(BF)


def input_high_kernel(gact_ref, xw_ref, dyw_ref, gain_ref, wq_ref, lon0_ref, gg0_ref, own_ref, lon_ref, gg_ref, win, dst):
    gain = gain_ref[...]
    acc = gg0_ref[...] + sum(input_rows(w, gact_ref, xw_ref, dyw_ref, gain, wq_ref, win) for w in (0, 1))
    for j in range(8):
        gg_ref[j : j + 1, :] = acc[:, j * 128 : (j + 1) * 128]
    lon_ref[0:48, :] = lon0_ref[...]
    dst[64:80, :] = jnp.zeros((16, D), F32)
    for at, here, size, _ in lon_out_segments(1):
        dst[at - 48 : at - 48 + size, :] = win[here : here + size, :]
    lon_ref[48:128, :] = dst[0:80, :].astype(BF)
    for own, here, size in own_segments():
        if slot(here) < 2:
            dst[own : own + size, :] = win[here : here + size, :]
    for lev in range(LEV):
        for r in range(3, 9):
            at = (lev * NR + r) * NC
            own_ref[lev, r - 3] = dst[at : at + NC, :].astype(BF)


def lon_out_segments(part):
    for lev in range(LEV):
        for rr in (range(6, 9), range(6))[part]:
            at = (48 + (lev * 6 + rr) * 6) if part else (lev * 3 + rr - 6) * 6
            yield at, window_row(lev, rr, 18), 6, (lev * NR + rr + 3) * NC


def input_low_call(gact, xw, dyw, gain, wq):
    return pl.pallas_call(
        input_low_kernel,
        out_shape=(
            jax.ShapeDtypeStruct((LEV, 3, NC, D), BF),
            jax.ShapeDtypeStruct((LATN, D), BF),
            jax.ShapeDtypeStruct((48, D), BF),
            jax.ShapeDtypeStruct((DIAGN, D), BF),
            jax.ShapeDtypeStruct((1, D), F32),
        ),
        scratch_shapes=[pltpu.VMEM((ROWS, D), F32), pltpu.VMEM((ROWS, D), F32)],
        compiler_params=params(24),
        cost_estimate=cost(1e9, 9e6),
        name="input_low",
    )(gact, xw, dyw, gain, wq)


def input_high_call(gact, xw, dyw, gain, wq, lon0, gg0):
    return pl.pallas_call(
        input_high_kernel,
        out_shape=(
            jax.ShapeDtypeStruct((LEV, 6, NC, D), BF),
            jax.ShapeDtypeStruct((128, D), BF),
            jax.ShapeDtypeStruct((8, 128), F32),
        ),
        scratch_shapes=[pltpu.VMEM((ROWS, D), F32), pltpu.VMEM((ROWS, D), F32)],
        compiler_params=params(24),
        cost_estimate=cost(1e9, 9e6),
        name="input_high",
    )(gact, xw, dyw, gain, wq, lon0, gg0)


def join_kernel(high_ref, low_ref, lat_ref, lon_ref, diag_ref, out_ref, src, dst):
    for lev in range(LEV):
        for r in range(3, NR):
            at = (lev * NR + r) * NC
            part = high_ref[lev, r - 3] if r < 9 else low_ref[lev, r - 9]
            dst[at : at + NC, :] = part.astype(F32)
    lon_parts = [*lon_out_segments(0), *lon_out_segments(1)]
    for halo, segments in ((lat_ref, lat_segments()), (lon_ref, lon_parts), (diag_ref, diag_segments())):
        count = halo.shape[0]
        src[:count, :] = halo[...].astype(F32)
        for here, _, size, own in segments:
            dst[own : own + size, :] = src[here : here + size, :]
    for lev in range(LEV):
        for r in range(NR):
            at = (lev * NR + r) * NC
            out_ref[lev, r] = dst[at : at + NC, :].astype(BF)


def join_call(high, low, lat, lon, diag):
    return pl.pallas_call(
        join_kernel,
        out_shape=jax.ShapeDtypeStruct((LEV, NR, NC, D), BF),
        scratch_shapes=[pltpu.VMEM((128, D), F32), pltpu.VMEM((ROWS, D), F32)],
        compiler_params=params(12),
        cost_estimate=cost(1e6, 4e6),
        name="join",
    )(high, low, lat, lon, diag)


MSG = 272


def x_of():
    return lax.axis_index("xh") * 2 + lax.axis_index("xl")


def x_block(x):
    return lax.rem(x, 2) * 2 + x // 2


def put_gain(out, at, gg):
    hi = gg.astype(BF)
    out[at : at + 16, :] = jnp.zeros((16, 512), BF)
    out[at : at + 8, 0:128] = hi
    out[at : at + 8, 128:256] = (gg - hi.astype(F32)).astype(BF)


def take_gain(ref, at):
    return ref[at : at + 8, 0:128].astype(F32) + ref[at : at + 8, 128:256].astype(F32)


def split_kernel(keep_ref, recv_ref, gg_ref, owna, a1, a2, a3, ownb, b1, b2, b3):
    y = lax.axis_index("y")
    x = x_of()

    def total(rows, cols):
        return keep_ref[rows, cols].astype(F32) + recv_ref[rows, cols].astype(F32)

    for k, out in enumerate((owna, a1, a2, a3)):
        rows = pl.ds(pl.multiple_of(lax.rem(y + k, 4) * 256, 256), 256)
        out[0:256, :] = total(rows, slice(0, 512)).astype(out.dtype)
        if k:
            put_gain(out, 256, gg_ref[...])
    for k, out in enumerate((ownb, b1, b2, b3)):
        block = x_block(lax.rem(x + k, 4))
        for j in range(4):
            rows = pl.ds(pl.multiple_of(j * 256 + block * 64, 64), 64)
            out[j * 64 : (j + 1) * 64, :] = total(rows, slice(512, 1024)).astype(out.dtype)


def split_call(keep, recv, gg):
    mine = jax.ShapeDtypeStruct((256, 512), F32)
    a = jax.ShapeDtypeStruct((MSG, 512), BF)
    b = jax.ShapeDtypeStruct((256, 512), BF)
    return pl.pallas_call(
        split_kernel,
        out_shape=(mine, a, a, a, mine, b, b, b),
        compiler_params=params(12),
        cost_estimate=cost(1e6, 8e6),
        name="split",
    )(keep, recv, gg)


def cross_kernel(owna, a1, a2, a3, ownb, b1, b2, b3, gg_ref, gout, nowna, na1, na2, na3, nownb, nb1, nb2, nb3):
    y = lax.axis_index("y")
    x = x_of()
    gg = gg_ref[...] + take_gain(a1, 256) + take_gain(a2, 256) + take_gain(a3, 256)
    gout[...] = gg

    def total(rows, own, refs):
        value = own[rows, :]
        for ref in refs:
            value += ref[rows, :].astype(F32)
        return value

    for k, out in enumerate((nowna, na1, na2, na3)):
        rows = pl.ds(pl.multiple_of(x_block(lax.rem(x + k, 4)) * 64, 64), 64)
        out[0:64, :] = total(rows, owna, (a1, a2, a3)).astype(out.dtype)
        if k:
            put_gain(out, 64, gg)
    for k, out in enumerate((nownb, nb1, nb2, nb3)):
        rows = pl.ds(pl.multiple_of(lax.rem(y + k, 4) * 64, 64), 64)
        out[...] = total(rows, ownb, (b1, b2, b3)).astype(out.dtype)


def cross_call(*operands):
    mine = jax.ShapeDtypeStruct((64, 512), F32)
    a = jax.ShapeDtypeStruct((80, 512), BF)
    b = jax.ShapeDtypeStruct((64, 512), BF)
    return pl.pallas_call(
        cross_kernel,
        out_shape=(jax.ShapeDtypeStruct((8, 128), F32), mine, a, a, a, mine, b, b, b),
        compiler_params=params(8),
        cost_estimate=cost(1e6, 4e6),
        name="cross",
    )(*operands)


def gather_kernel(owna, a1, a2, a3, ownb, b1, b2, b3, gg_ref, out_ref):
    gg = gg_ref[...] + take_gain(a1, 64) + take_gain(a2, 64) + take_gain(a3, 64)
    gg = gg.astype(BF)
    for i in range(8):
        rows = slice(i * 8, (i + 1) * 8)
        parts = []
        for own, refs in ((owna, (a1, a2, a3)), (ownb, (b1, b2, b3))):
            value = own[rows, :]
            for ref in refs:
                value += ref[rows, :].astype(F32)
            parts.append(value)
        for j in range(2):
            half = slice(j * 4, j * 4 + 4)
            out_ref[2 * i + j, :, 0:512] = jnp.concatenate([parts[0][half], parts[1][half]], 0).astype(BF)
            out_ref[2 * i + j, :, 512:640] = gg


def gather_call(*operands):
    return pl.pallas_call(
        gather_kernel,
        out_shape=jax.ShapeDtypeStruct((16, 8, 640), BF),
        compiler_params=params(6),
        cost_estimate=cost(1e6, 4e6),
        name="gather",
    )(*operands)


def final_kernel(blocks, wq_ref, wp_ref, gain_ref, gg):
    low = jnp.zeros((8, 640), F32)
    high = jnp.zeros((8, 640), F32)
    for z in range(8):
        low += blocks[2 * z].astype(F32)
        high += blocks[2 * z + 1].astype(F32)
    low = low * FACTOR
    high = high * FACTOR
    wq_ref[:, 0:512] = low[0:4, 0:512]
    wq_ref[:, 512:1024] = low[4:8, 0:512]
    wq_ref[:, 1024:1536] = high[0:4, 0:512]
    wp_ref[...] = high[4:8, 0:512]
    gg[...] = low[:, 512:640] + high[:, 512:640]
    device = lax.axis_index("y") * 64 + lax.axis_index("xl") * 32 + lax.axis_index("xh") * 16
    device = device + lax.axis_index("z") * 2 + lax.axis_index("c")
    row = gg[pl.ds(device // 32, 1), :]
    gain_ref[...] = pltpu.roll(row, lax.rem(128 - lax.rem(device, 32) * 4, 128), 1)[:, 0:4]


def final_call(blocks):
    return pl.pallas_call(
        final_kernel,
        out_shape=(
            jax.ShapeDtypeStruct((4, 1536), F32),
            jax.ShapeDtypeStruct((4, HH), F32),
            jax.ShapeDtypeStruct((1, 4), F32),
        ),
        scratch_shapes=[pltpu.VMEM((8, 128), F32)],
        compiler_params=params(4),
        cost_estimate=cost(1e6, 1e6),
        name="final",
    )(blocks)


def shift_x(value, k):
    pairs = []
    for xl in range(2):
        for xh in range(2):
            to = (xh * 2 + xl + k) % 4
            pairs.append((xl * 2 + xh, (to % 2) * 2 + to // 2))
    return lax.ppermute(value, ("xl", "xh"), pairs)


def shift_y(value, k):
    return lax.ppermute(value, "y", shift(4, k))


def shift(n, k):
    return [(i, (i + k) % n) for i in range(n)]


def shift_both(k):
    pairs = []
    for i in range(8):
        for j in range(32):
            pairs.append((i * 32 + j, ((i + k) % 8) * 32 + (j + k) % 32))
    return pairs


LAT = ("y", "xl")
LON = ("xh", "z", "c")
ALL = LAT + LON


def program(x, dy, gain, wq, wp):
    gain2 = gain.reshape(1, D)
    lat, lon, diag = pack(x, dy)
    lon = lax.ppermute(lon, LON, shift(32, -1))
    lat = lax.ppermute(lat, LAT, shift(8, -1))
    diag = lax.ppermute(diag, ALL, shift_both(-1))
    early = early_call(0, x, dy, gain2, wq, wp)
    lon, first = lax.optimization_barrier((lon, early[0]))
    early = (first, *early[1:], *early_call(1, x, dy, lon, gain2, wq, wp))
    keep, send, gact, xw, dyw = main_call(x, dy, lat, lon, diag, gain2, wq, wp, *early)
    recv = lax.ppermute(send, "c", [(0, 1), (1, 0)])
    low, lat, lon0, diag, gg0 = input_low_call(gact, xw, dyw, gain2, wq)
    high, lon, gg = input_high_call(gact, xw, dyw, gain2, wq, lon0, gg0)
    oa, a1, a2, a3, ob, b1, b2, b3 = split_call(keep, recv, gg)
    a1, a2, a3 = (shift_y(v, k) for k, v in ((1, a1), (2, a2), (3, a3)))
    b1, b2, b3 = (shift_x(v, k) for k, v in ((1, b1), (2, b2), (3, b3)))
    lat = lax.ppermute(lat, LAT, shift(8, 1))
    lon = lax.ppermute(lon, LON, shift(32, 1))
    diag = lax.ppermute(diag, ALL, shift_both(1))
    gg, oa, a1, a2, a3, ob, b1, b2, b3 = cross_call(oa, a1, a2, a3, ob, b1, b2, b3, gg)
    a1, a2, a3 = (shift_x(v, k) for k, v in ((1, a1), (2, a2), (3, a3)))
    b1, b2, b3 = (shift_y(v, k) for k, v in ((1, b1), (2, b2), (3, b3)))
    grad_in = join_call(high, low, lat, lon, diag)
    a1, grad_in = lax.optimization_barrier((a1, grad_in))
    blocks = gather_call(oa, a1, a2, a3, ob, b1, b2, b3, gg)
    blocks = lax.all_to_all(blocks, ("z", "c"), 0, 0, tiled=True)
    grad_qkv, grad_proj, grad_gain = final_call(blocks)
    return grad_in, grad_qkv, grad_proj.T, grad_gain.reshape(4)


def solution(mesh):
    mesh = Mesh(mesh.devices.reshape(4, 2, 2, 8, 2), ALL)
    return jax.shard_map(
        program,
        mesh=mesh,
        in_specs=(P(None, LAT, LON, None), P(None, LAT, LON, None), P(), P(), P()),
        out_specs=(P(None, LAT, LON, None), P(ALL, None), P(None, ALL), P(ALL)),
        check_vma=False,
    )
```

profile of v0, /device:TPU:1, one launch (start us, length us, event | category | flops | bytes accessed | tf_op | source)
XLA Modules:
  0.0 98.3 jit_solution(14512119192951192243)
XLA Ops:
  0.7 2.7 %pack.1 = (bf16[2,112,1024]{2,1,0:T(8,128)(2,1)}, bf16[2,112,1024]{2,1,0:T(8,128)(2,1)}, bf16[2,48,1024]{2,1,0:T(8,128)(2,1)}) custom-call(bf16[2,12,24,1024]{3,2,1,0:T(8,128)(2,1)} %x_ref.7, bf16[2,12,24,1024]{3,2,1,0:T(8,128)(2,1)} %dy_ref.7), custom_call_target="tpu_custom_call" | custom-call | flops 1000000 | bytes 4000000 | tf_op jit(solution)/shard_map/pack/pallas_call | solution.py:106
  3.4 3.3 %collective-permute-start.1 = (bf16[2,112,1024]{2,1,0:T(8,128)(2,1)}, bf16[2,112,1024]{2,1,0:T(8,128)(2,1)S(1)}, u32[]{:S(2)}, u32[]{:S(2)}) collective-permute-start(bf16[2,112,1024]{2,1,0:T(8,128)(2,1)} %get-tuple-element.53), channel_id=1, source_target_pairs={{0,31},{1,0},{2,1},{3,2},{4,3},{5,4},{6,5},{7,6},{8,7},{9,8},{10,9... | collective-permute-start | bytes 1376264 | tf_op jit(solution)/shard_map/ppermute | solution.py:595
  6.6 2.0 %collective-permute-start = (bf16[2,112,1024]{2,1,0:T(8,128)(2,1)}, bf16[2,112,1024]{2,1,0:T(8,128)(2,1)S(1)}, u32[]{:S(2)}, u32[]{:S(2)}) collective-permute-start(bf16[2,112,1024]{2,1,0:T(8,128)(2,1)} %get-tuple-element.52), channel_id=1, source_target_pairs={{0,224},{32,0},{64,32},{96,64},{128,96},{160,128},{192,160},{224,1... | collective-permute-start | bytes 1376264 | tf_op jit(solution)/shard_map/ppermute | solution.py:596
  8.6 8.2 %collective-permute-start.2 = (bf16[2,48,1024]{2,1,0:T(8,128)(2,1)}, bf16[2,48,1024]{2,1,0:T(8,128)(2,1)S(1)}, u32[]{:S(2)}, u32[]{:S(2)}) collective-permute-start(bf16[2,48,1024]{2,1,0:T(8,128)(2,1)} %get-tuple-element.56), channel_id=1, source_target_pairs={{0,255},{1,224},{2,225},{3,226},{4,227},{5,228},{6,229},{7,230},{8... | collective-permute-start | bytes 589832 | tf_op jit(solution)/shard_map/ppermute | solution.py:597
  16.8 1.9 %copy-done = bf16[1024,1536]{1,0:T(8,128)(2,1)S(1)} copy-done((bf16[1024,1536]{1,0:T(8,128)(2,1)S(1)}, bf16[1024,1536]{1,0:T(8,128)(2,1)}, u32[]{:S(2)}) %copy-start) | copy-done | bytes 3145752
  18.7 1.2 %copy-done.5 = bf16[512,1024]{1,0:T(8,128)(2,1)S(1)} copy-done((bf16[512,1024]{1,0:T(8,128)(2,1)S(1)}, bf16[512,1024]{1,0:T(8,128)(2,1)}, u32[]{:S(2)}) %copy-start.5) | copy-done | bytes 1048600
  19.9 3.3 %shard_map.84 = (bf16[144,1024]{1,0:T(8,128)(2,1)S(1)}, bf16[144,1024]{1,0:T(8,128)(2,1)S(1)}, bf16[144,1024]{1,0:T(8,128)(2,1)S(1)}, bf16[144,2048]{1,0:T(8,128)(2,1)S(1)}) custom-call(bf16[2,12,24,1024]{3,2,1,0:T(8,128)(2,1)S(1)} %copy-done.2, bf16[2,12,24,1024]{3,2,1,0:T(8,128)(2,1)S(1)} %copy-done.3, f32[1,1024]{1,0:T(1,128)S(1)} %bitcast.3, ...), custom_call_target="tpu_custom_call" | custom-call | flops 2000000000 | bytes 9000000 | tf_op jit(solution)/shard_map/pallas_call | solution.py:221
  23.2 0.0 collective-permute-done.1.refs_0_.lon_ref
  23.2 0.0 copy-start.1
  23.3 0.0 copy-start.6
  23.3 3.3 %shard_map.85 = (bf16[144,1024]{1,0:T(8,128)(2,1)S(1)}, bf16[144,1024]{1,0:T(8,128)(2,1)S(1)}, bf16[144,1024]{1,0:T(8,128)(2,1)S(1)}, bf16[144,2048]{1,0:T(8,128)(2,1)S(1)}) custom-call(bf16[2,12,24,1024]{3,2,1,0:T(8,128)(2,1)S(1)} %copy-done.2, bf16[2,12,24,1024]{3,2,1,0:T(8,128)(2,1)S(1)} %copy-done.3, ...), custom_call_target="tpu_custom_call" | custom-call | flops 2000000000 | bytes 9000000 | tf_op jit(solution)/shard_map/pallas_call | solution.py:221
  26.6 0.0 collective-permute-done.2.diag_ref
  26.6 0.0 collective-permute-done.lat_ref
  26.6 10.0 %main.1 = (bf16[1024,1024]{1,0:T(8,128)(2,1)S(1)}, bf16[1024,1024]{1,0:T(8,128)(2,1)S(1)}, bf16[576,2048]{1,0:T(8,128)(2,1)S(1)}, bf16[576,1024]{1,0:T(8,128)(2,1)S(1)}, bf16[576,1024]{1,0:T(8,128)(2,1)S(1)}) custom-call(bf16[2,12,24,1024]{3,2,1,0:T(8,128)(2,1)S(1)} %copy-done.2, bf16[2,12,24,1024]{3,2,1,0:T(8,128)(2,1)S(1)} %copy-done.3, ...), custom_call_target="tpu_custom_call" | custom-call | flops 5500000256 | bytes 14000000 | tf_op jit(solution)/shard_map/main/pallas_call | solution.py:270
  36.6 0.1 collective-permute-start.3
  36.7 2.8 %input_low.1 = (bf16[2,3,24,1024]{3,2,1,0:T(8,128)(2,1)S(1)}, bf16[112,1024]{1,0:T(8,128)(2,1)S(1)}, bf16[48,1024]{1,0:T(8,128)(2,1)S(1)}, bf16[48,1024]{1,0:T(8,128)(2,1)S(1)}, f32[1,1024]{1,0:T(1,128)S(1)}) custom-call(bf16[576,2048]{1,0:T(8,128)(2,1)S(1)} %get-tuple-element.67.gact_ref, bf16[576,1024]{1,0:T(8,128)(2,1)S(1)} %get-tuple-element.68.xw_ref, ...), custom_call_target="tpu_custom_call" | custom-call | flops 1000000000 | bytes 9000000 | tf_op jit(solution)/shard_map/input_low/pallas_call | solution.py:352
  39.5 2.8 %input_high.1 = (bf16[2,6,24,1024]{3,2,1,0:T(8,128)(2,1)S(1)}, bf16[128,1024]{1,0:T(8,128)(2,1)S(1)}, f32[8,128]{1,0:T(8,128)S(1)}) custom-call(bf16[576,2048]{1,0:T(8,128)(2,1)S(1)} %get-tuple-element.67.gact_ref, bf16[576,1024]{1,0:T(8,128)(2,1)S(1)} %get-tuple-element.68.xw_ref, bf16[576,1024]{1,0:T(8,128)(2,1)S(1)} %get-tuple-element.69.dyw_ref, ...), custom_call_target="tpu_custom_call" | custom-call | flops 1000000000 | bytes 9000000 | tf_op jit(solution)/shard_map/input_high/pallas_call | solution.py:369
  42.4 0.5 split.1
  42.9 0.4 collective-permute-start.7
  43.3 1.7 %collective-permute-start.8 = (bf16[256,512]{1,0:T(8,128)(2,1)S(1)}, bf16[256,512]{1,0:T(8,128)(2,1)S(1)}, u32[]{:S(2)}, u32[]{:S(2)}) collective-permute-start(bf16[256,512]{1,0:T(8,128)(2,1)S(1)} %get-tuple-element.79), channel_id=1, source_target_pairs={{0,16},{16,0},{32,48},{48,32},{1,17},{17,1},{33,49},{49,33},{2,18}... | collective-permute-start | bytes 786440 | tf_op jit(solution)/shard_map/ppermute | solution.py:568
  45.0 0.8 collective-permute-start.9
  45.8 0.0 collective-permute-start.4
  45.8 2.9 %collective-permute-start.5 = (bf16[272,512]{1,0:T(8,128)(2,1)S(1)}, bf16[272,512]{1,0:T(8,128)(2,1)S(1)}, u32[]{:S(2)}, u32[]{:S(2)}) collective-permute-start(bf16[272,512]{1,0:T(8,128)(2,1)S(1)} %get-tuple-element.75), channel_id=1, source_target_pairs={{0,128},{64,192},{128,0},{192,64},{1,129},{65,193},{129,1},{193,65... | collective-permute-start | bytes 835592 | tf_op jit(solution)/shard_map/ppermute | solution.py:572
  48.6 3.5 %collective-permute-done.7.b1 = bf16[256,512]{1,0:T(8,128)(2,1)S(1)} collective-permute-done((bf16[256,512]{1,0:T(8,128)(2,1)S(1)}, bf16[256,512]{1,0:T(8,128)(2,1)S(1)}, u32[]{:S(2)}, u32[]{:S(2)}) %collective-permute-start.7) | collective-permute-done | bytes 262176 | tf_op jit(solution)/shard_map/ppermute | solution.py:568
  52.1 4.4 %collective-permute-done.8.b2 = bf16[256,512]{1,0:T(8,128)(2,1)S(1)} collective-permute-done((bf16[256,512]{1,0:T(8,128)(2,1)S(1)}, bf16[256,512]{1,0:T(8,128)(2,1)S(1)}, u32[]{:S(2)}, u32[]{:S(2)}) %collective-permute-start.8) | collective-permute-done | bytes 262176 | tf_op jit(solution)/shard_map/ppermute | solution.py:568
  56.5 1.0 %collective-permute-start.12 = (bf16[128,1024]{1,0:T(8,128)(2,1)S(1)}, bf16[128,1024]{1,0:T(8,128)(2,1)S(1)}, u32[]{:S(2)}, u32[]{:S(2)}) collective-permute-start(bf16[128,1024]{1,0:T(8,128)(2,1)S(1)} %get-tuple-element.85), channel_id=1, source_target_pairs={{0,1},{1,2},{2,3},{3,4},{4,5},{5,6},{6,7},{7,8},{8,9},{9,10},{10,1... | collective-permute-start | bytes 786440 | tf_op jit(solution)/shard_map/ppermute | solution.py:609
  57.6 0.0 collective-permute-done.9.b3
  57.6 1.1 %collective-permute-start.11 = (bf16[112,1024]{1,0:T(8,128)(2,1)S(1)}, bf16[112,1024]{1,0:T(8,128)(2,1)S(1)}, u32[]{:S(2)}, u32[]{:S(2)}) collective-permute-start(bf16[112,1024]{1,0:T(8,128)(2,1)S(1)} %get-tuple-element.84), channel_id=1, source_target_pairs={{0,32},{32,64},{64,96},{96,128},{128,160},{160,192},{192,224},{224... | collective-permute-start | bytes 688136 | tf_op jit(solution)/shard_map/ppermute | solution.py:608
  58.7 1.3 %collective-permute-start.13 = (bf16[48,1024]{1,0:T(8,128)(2,1)S(1)}, bf16[48,1024]{1,0:T(8,128)(2,1)S(1)}, u32[]{:S(2)}, u32[]{:S(2)}) collective-permute-start(bf16[48,1024]{1,0:T(8,128)(2,1)S(1)} %get-tuple-element.86), channel_id=1, source_target_pairs={{0,33},{1,34},{2,35},{3,36},{4,37},{5,38},{6,39},{7,40},{8,41},{9,... | collective-permute-start | bytes 294920 | tf_op jit(solution)/shard_map/ppermute | solution.py:610
  60.1 0.7 collective-permute-done.5.a2
  60.8 0.3 cross.1
  61.0 0.9 collective-permute-start.10
  61.9 1.8 %collective-permute-start.14 = (bf16[80,512]{1,0:T(8,128)(2,1)S(1)}, bf16[80,512]{1,0:T(8,128)(2,1)S(1)}, u32[]{:S(2)}, u32[]{:S(2)}) collective-permute-start(bf16[80,512]{1,0:T(8,128)(2,1)S(1)} %get-tuple-element.90), channel_id=1, source_target_pairs={{0,16},{16,0},{32,48},{48,32},{1,17},{17,1},{33,49},{49,33},{2,18}... | collective-permute-start | bytes 245768 | tf_op jit(solution)/shard_map/ppermute | solution.py:568
  63.7 8.4 %collective-permute-done.13.diag_ref = bf16[48,1024]{1,0:T(8,128)(2,1)S(1)} collective-permute-done((bf16[48,1024]{1,0:T(8,128)(2,1)S(1)}, bf16[48,1024]{1,0:T(8,128)(2,1)S(1)}, u32[]{:S(2)}, u32[]{:S(2)}) %collective-permute-start.13) | collective-permute-done | bytes 98336 | tf_op jit(solution)/shard_map/ppermute | solution.py:610
  72.1 1.5 %collective-permute-start.15 = (bf16[80,512]{1,0:T(8,128)(2,1)S(1)}, bf16[80,512]{1,0:T(8,128)(2,1)S(1)}, u32[]{:S(2)}, u32[]{:S(2)}) collective-permute-start(bf16[80,512]{1,0:T(8,128)(2,1)S(1)} %get-tuple-element.91), channel_id=1, source_target_pairs={{0,48},{16,32},{32,0},{48,16},{1,49},{17,33},{33,1},{49,17},{2,50}... | collective-permute-start | bytes 245768 | tf_op jit(solution)/shard_map/ppermute | solution.py:568
  73.6 0.0 collective-permute-done.11.lat_ref
  73.6 0.0 collective-permute-start.16
  73.6 0.0 collective-permute-done.12.lon_ref
  73.6 2.6 %collective-permute-start.17 = (bf16[64,512]{1,0:T(8,128)(2,1)S(1)}, bf16[64,512]{1,0:T(8,128)(2,1)S(1)}, u32[]{:S(2)}, u32[]{:S(2)}) collective-permute-start(bf16[64,512]{1,0:T(8,128)(2,1)S(1)} %get-tuple-element.94), channel_id=1, source_target_pairs={{0,128},{64,192},{128,0},{192,64},{1,129},{65,193},{129,1},{193,65... | collective-permute-start | bytes 196616 | tf_op jit(solution)/shard_map/ppermute | solution.py:572
  76.2 0.0 collective-permute-done.10.a1
  76.3 0.1 collective-permute-start.18
  76.4 1.5 %join.1 = bf16[2,12,24,1024]{3,2,1,0:T(8,128)(2,1)} custom-call(bf16[2,6,24,1024]{3,2,1,0:T(8,128)(2,1)S(1)} %get-tuple-element.82.high_ref, bf16[2,3,24,1024]{3,2,1,0:T(8,128)(2,1)S(1)} %get-tuple-element.83.low_ref, bf16[112,1024]{1,0:T(8,128)(2,1)S(1)} %collective-permute-done.11.lat_ref, bf16[128,1024]{1,0:T(8,128)(2,1)S(1)} %collective-permute-done.12.lon_ref, ...), custom_call_target="tpu_custom_call" | custom-call | flops 1000000 | bytes 4000000 | tf_op jit(solution)/shard_map/join/pallas_call | solution.py:402
  77.8 0.1 collective-permute-done.16.b1
  77.9 0.7 collective-permute-done.17.b2
  78.6 1.0 collective-permute-done.18.b3
  79.6 0.1 gather.1
  79.7 17.9 %all_to_all.5.blocks = bf16[16,8,640]{2,1,0:T(8,128)(2,1)S(1)} all-to-all(bf16[16,8,640]{2,1,0:T(8,128)(2,1)S(1)} %gather.1), channel_id=1, replica_groups=mesh['y'=4,'xl'=2,'xh'=2,'z'=8,'c'=2] {'z','c'}, dimensions={0} | all-to-all | bytes 327680 | tf_op jit(solution)/shard_map/all_to_all | solution.py:617
  97.7 0.6 final.1
  (16 shorter events, 0.0 us)
Async XLA Ops:
  0.6 16.1 %copy-start.3 = (bf16[2,12,24,1024]{3,2,1,0:T(8,128)(2,1)S(1)}, bf16[2,12,24,1024]{3,2,1,0:T(8,128)(2,1)}, u32[]{:S(2)}) copy-start(bf16[2,12,24,1024]{3,2,1,0:T(8,128)(2,1)} %dy_ref.7) | copy-start | bytes 3538948
  0.6 16.1 %copy-start.2 = (bf16[2,12,24,1024]{3,2,1,0:T(8,128)(2,1)S(1)}, bf16[2,12,24,1024]{3,2,1,0:T(8,128)(2,1)}, u32[]{:S(2)}) copy-start(bf16[2,12,24,1024]{3,2,1,0:T(8,128)(2,1)} %x_ref.7) | copy-start | bytes 3538948
  0.7 16.1 %copy-start.4 = (f32[1024]{0:T(1024)S(1)}, f32[1024]{0:T(1024)}, u32[]{:S(2)}) copy-start(f32[1024]{0:T(1024)} %param.7) | copy-start | bytes 12292
  3.4 19.9 %collective-permute-start.1 = (bf16[2,112,1024]{2,1,0:T(8,128)(2,1)}, bf16[2,112,1024]{2,1,0:T(8,128)(2,1)S(1)}, u32[]{:S(2)}, u32[]{:S(2)}) collective-permute-start(bf16[2,112,1024]{2,1,0:T(8,128)(2,1)} %get-tuple-element.53), channel_id=1, source_target_pairs={{0,31},{1,0},{2,1},{3,2},{4,3},{5,4},{6,5},{7,6},{8,7},{9,8},{10,9... | collective-permute-start | bytes 1376264 | tf_op jit(solution)/shard_map/ppermute | solution.py:595
  6.6 20.0 %collective-permute-start = (bf16[2,112,1024]{2,1,0:T(8,128)(2,1)}, bf16[2,112,1024]{2,1,0:T(8,128)(2,1)S(1)}, u32[]{:S(2)}, u32[]{:S(2)}) collective-permute-start(bf16[2,112,1024]{2,1,0:T(8,128)(2,1)} %get-tuple-element.52), channel_id=1, source_target_pairs={{0,224},{32,0},{64,32},{96,64},{128,96},{160,128},{192,160},{224,1... | collective-permute-start | bytes 1376264 | tf_op jit(solution)/shard_map/ppermute | solution.py:596
  8.6 18.0 %collective-permute-start.2 = (bf16[2,48,1024]{2,1,0:T(8,128)(2,1)}, bf16[2,48,1024]{2,1,0:T(8,128)(2,1)S(1)}, u32[]{:S(2)}, u32[]{:S(2)}) collective-permute-start(bf16[2,48,1024]{2,1,0:T(8,128)(2,1)} %get-tuple-element.56), channel_id=1, source_target_pairs={{0,255},{1,224},{2,225},{3,226},{4,227},{5,228},{6,229},{7,230},{8... | collective-permute-start | bytes 589832 | tf_op jit(solution)/shard_map/ppermute | solution.py:597
  16.8 1.9 %copy-start = (bf16[1024,1536]{1,0:T(8,128)(2,1)S(1)}, bf16[1024,1536]{1,0:T(8,128)(2,1)}, u32[]{:S(2)}) copy-start(bf16[1024,1536]{1,0:T(8,128)(2,1)} %wq_ref.5) | copy-start | bytes 9437188
  18.7 1.2 %copy-start.5 = (bf16[512,1024]{1,0:T(8,128)(2,1)S(1)}, bf16[512,1024]{1,0:T(8,128)(2,1)}, u32[]{:S(2)}) copy-start(bf16[512,1024]{1,0:T(8,128)(2,1)} %wp_ref.1) | copy-start | bytes 3145732
  23.2 3.4 %copy-start.1 = (bf16[1024,1536]{1,0:T(8,128)(2,1)S(1)}, bf16[1024,1536]{1,0:T(8,128)(2,1)}, u32[]{:S(2)}) copy-start(bf16[1024,1536]{1,0:T(8,128)(2,1)} %wq_ref.5) | copy-start | bytes 9437188
  23.3 3.4 %copy-start.6 = (bf16[512,1024]{1,0:T(8,128)(2,1)S(1)}, bf16[512,1024]{1,0:T(8,128)(2,1)}, u32[]{:S(2)}) copy-start(bf16[512,1024]{1,0:T(8,128)(2,1)} %wp_ref.1) | copy-start | bytes 3145732
  36.6 5.7 %collective-permute-start.3 = (bf16[1024,1024]{1,0:T(8,128)(2,1)S(1)}, bf16[1024,1024]{1,0:T(8,128)(2,1)S(1)}, u32[]{:S(2)}, u32[]{:S(2)}) collective-permute-start(bf16[1024,1024]{1,0:T(8,128)(2,1)S(1)} %get-tuple-element.66), channel_id=1, source_target_pairs={{0,1},{1,0},{2,3},{3,2},{4,5},{5,4},{6,7},{7,6},{8,9},{9,8},{10,11... | collective-permute-start | bytes 6291464 | tf_op jit(solution)/shard_map/ppermute | solution.py:602
  42.9 9.3 %collective-permute-start.7 = (bf16[256,512]{1,0:T(8,128)(2,1)S(1)}, bf16[256,512]{1,0:T(8,128)(2,1)S(1)}, u32[]{:S(2)}, u32[]{:S(2)}) collective-permute-start(bf16[256,512]{1,0:T(8,128)(2,1)S(1)} %get-tuple-element.78), channel_id=1, source_target_pairs={{0,32},{16,48},{32,16},{48,0},{1,33},{17,49},{33,17},{49,1},{2,34}... | collective-permute-start | bytes 786440 | tf_op jit(solution)/shard_map/ppermute | solution.py:568
  43.3 13.3 %collective-permute-start.8 = (bf16[256,512]{1,0:T(8,128)(2,1)S(1)}, bf16[256,512]{1,0:T(8,128)(2,1)S(1)}, u32[]{:S(2)}, u32[]{:S(2)}) collective-permute-start(bf16[256,512]{1,0:T(8,128)(2,1)S(1)} %get-tuple-element.79), channel_id=1, source_target_pairs={{0,16},{16,0},{32,48},{48,32},{1,17},{17,1},{33,49},{49,33},{2,18}... | collective-permute-start | bytes 786440 | tf_op jit(solution)/shard_map/ppermute | solution.py:568
  45.0 12.6 %collective-permute-start.9 = (bf16[256,512]{1,0:T(8,128)(2,1)S(1)}, bf16[256,512]{1,0:T(8,128)(2,1)S(1)}, u32[]{:S(2)}, u32[]{:S(2)}) collective-permute-start(bf16[256,512]{1,0:T(8,128)(2,1)S(1)} %get-tuple-element.80), channel_id=1, source_target_pairs={{0,48},{16,32},{32,0},{48,16},{1,49},{17,33},{33,1},{49,17},{2,50}... | collective-permute-start | bytes 786440 | tf_op jit(solution)/shard_map/ppermute | solution.py:568
  45.8 13.0 %collective-permute-start.4 = (bf16[272,512]{1,0:T(8,128)(2,1)S(1)}, bf16[272,512]{1,0:T(8,128)(2,1)S(1)}, u32[]{:S(2)}, u32[]{:S(2)}) collective-permute-start(bf16[272,512]{1,0:T(8,128)(2,1)S(1)} %get-tuple-element.74), channel_id=1, source_target_pairs={{0,64},{64,128},{128,192},{192,0},{1,65},{65,129},{129,193},{193,1... | collective-permute-start | bytes 835592 | tf_op jit(solution)/shard_map/ppermute | solution.py:572
  45.8 15.0 %collective-permute-start.5 = (bf16[272,512]{1,0:T(8,128)(2,1)S(1)}, bf16[272,512]{1,0:T(8,128)(2,1)S(1)}, u32[]{:S(2)}, u32[]{:S(2)}) collective-permute-start(bf16[272,512]{1,0:T(8,128)(2,1)S(1)} %get-tuple-element.75), channel_id=1, source_target_pairs={{0,128},{64,192},{128,0},{192,64},{1,129},{65,193},{129,1},{193,65... | collective-permute-start | bytes 835592 | tf_op jit(solution)/shard_map/ppermute | solution.py:572
  52.1 8.6 %collective-permute-start.6 = (bf16[272,512]{1,0:T(8,128)(2,1)S(1)}, bf16[272,512]{1,0:T(8,128)(2,1)S(1)}, u32[]{:S(2)}, u32[]{:S(2)}) collective-permute-start(bf16[272,512]{1,0:T(8,128)(2,1)S(1)} %get-tuple-element.76), channel_id=1, source_target_pairs={{0,192},{64,0},{128,64},{192,128},{1,193},{65,1},{129,65},{193,129... | collective-permute-start | bytes 835592 | tf_op jit(solution)/shard_map/ppermute | solution.py:572
  56.5 17.1 %collective-permute-start.12 = (bf16[128,1024]{1,0:T(8,128)(2,1)S(1)}, bf16[128,1024]{1,0:T(8,128)(2,1)S(1)}, u32[]{:S(2)}, u32[]{:S(2)}) collective-permute-start(bf16[128,1024]{1,0:T(8,128)(2,1)S(1)} %get-tuple-element.85), channel_id=1, source_target_pairs={{0,1},{1,2},{2,3},{3,4},{4,5},{5,6},{6,7},{7,8},{8,9},{9,10},{10,1... | collective-permute-start | bytes 786440 | tf_op jit(solution)/shard_map/ppermute | solution.py:609
  57.6 16.0 %collective-permute-start.11 = (bf16[112,1024]{1,0:T(8,128)(2,1)S(1)}, bf16[112,1024]{1,0:T(8,128)(2,1)S(1)}, u32[]{:S(2)}, u32[]{:S(2)}) collective-permute-start(bf16[112,1024]{1,0:T(8,128)(2,1)S(1)} %get-tuple-element.84), channel_id=1, source_target_pairs={{0,32},{32,64},{64,96},{96,128},{128,160},{160,192},{192,224},{224... | collective-permute-start | bytes 688136 | tf_op jit(solution)/shard_map/ppermute | solution.py:608
  58.7 13.4 %collective-permute-start.13 = (bf16[48,1024]{1,0:T(8,128)(2,1)S(1)}, bf16[48,1024]{1,0:T(8,128)(2,1)S(1)}, u32[]{:S(2)}, u32[]{:S(2)}) collective-permute-start(bf16[48,1024]{1,0:T(8,128)(2,1)S(1)} %get-tuple-element.86), channel_id=1, source_target_pairs={{0,33},{1,34},{2,35},{3,36},{4,37},{5,38},{6,39},{7,40},{8,41},{9,... | collective-permute-start | bytes 294920 | tf_op jit(solution)/shard_map/ppermute | solution.py:610
  61.0 15.2 %collective-permute-start.10 = (bf16[80,512]{1,0:T(8,128)(2,1)S(1)}, bf16[80,512]{1,0:T(8,128)(2,1)S(1)}, u32[]{:S(2)}, u32[]{:S(2)}) collective-permute-start(bf16[80,512]{1,0:T(8,128)(2,1)S(1)} %get-tuple-element.81), channel_id=1, source_target_pairs={{0,32},{16,48},{32,16},{48,0},{1,33},{17,49},{33,17},{49,1},{2,34}... | collective-permute-start | bytes 245768 | tf_op jit(solution)/shard_map/ppermute | solution.py:568
  61.9 17.7 %collective-permute-start.14 = (bf16[80,512]{1,0:T(8,128)(2,1)S(1)}, bf16[80,512]{1,0:T(8,128)(2,1)S(1)}, u32[]{:S(2)}, u32[]{:S(2)}) collective-permute-start(bf16[80,512]{1,0:T(8,128)(2,1)S(1)} %get-tuple-element.90), channel_id=1, source_target_pairs={{0,16},{16,0},{32,48},{48,32},{1,17},{17,1},{33,49},{49,33},{2,18}... | collective-permute-start | bytes 245768 | tf_op jit(solution)/shard_map/ppermute | solution.py:568
  72.1 7.5 %collective-permute-start.15 = (bf16[80,512]{1,0:T(8,128)(2,1)S(1)}, bf16[80,512]{1,0:T(8,128)(2,1)S(1)}, u32[]{:S(2)}, u32[]{:S(2)}) collective-permute-start(bf16[80,512]{1,0:T(8,128)(2,1)S(1)} %get-tuple-element.91), channel_id=1, source_target_pairs={{0,48},{16,32},{32,0},{48,16},{1,49},{17,33},{33,1},{49,17},{2,50}... | collective-permute-start | bytes 245768 | tf_op jit(solution)/shard_map/ppermute | solution.py:568
  73.6 4.3 %collective-permute-start.16 = (bf16[64,512]{1,0:T(8,128)(2,1)S(1)}, bf16[64,512]{1,0:T(8,128)(2,1)S(1)}, u32[]{:S(2)}, u32[]{:S(2)}) collective-permute-start(bf16[64,512]{1,0:T(8,128)(2,1)S(1)} %get-tuple-element.93), channel_id=1, source_target_pairs={{0,64},{64,128},{128,192},{192,0},{1,65},{65,129},{129,193},{193,1... | collective-permute-start | bytes 196616 | tf_op jit(solution)/shard_map/ppermute | solution.py:572
  73.6 5.0 %collective-permute-start.17 = (bf16[64,512]{1,0:T(8,128)(2,1)S(1)}, bf16[64,512]{1,0:T(8,128)(2,1)S(1)}, u32[]{:S(2)}, u32[]{:S(2)}) collective-permute-start(bf16[64,512]{1,0:T(8,128)(2,1)S(1)} %get-tuple-element.94), channel_id=1, source_target_pairs={{0,128},{64,192},{128,0},{192,64},{1,129},{65,193},{129,1},{193,65... | collective-permute-start | bytes 196616 | tf_op jit(solution)/shard_map/ppermute | solution.py:572
  76.3 3.4 %collective-permute-start.18 = (bf16[64,512]{1,0:T(8,128)(2,1)S(1)}, bf16[64,512]{1,0:T(8,128)(2,1)S(1)}, u32[]{:S(2)}, u32[]{:S(2)}) collective-permute-start(bf16[64,512]{1,0:T(8,128)(2,1)S(1)} %get-tuple-element.95), channel_id=1, source_target_pairs={{0,192},{64,0},{128,64},{192,128},{1,193},{65,1},{129,65},{193,129... | collective-permute-start | bytes 196616 | tf_op jit(solution)/shard_map/ppermute | solution.py:572
where the time goes:
time: 98.5 us; the launch traced here: 98.3 us
  starting transfers between devices  29.7 us (30%)
  Pallas kernels  27.9 us (28%)
  waiting for transfers between devices  18.8 us (19%)
  blocking collectives  17.9 us (18%)
  local copies, waits for them, and re-layouts  3.13 us (3%)
    all_to_all x1, blocking collectives, program(): blocks = lax.all_to_all(blocks, ('z', 'c'), 0, 0, tiled=True)  17.9 us
    pallas_call x1, Pallas kernels, main_call(): pl.pallas_call(main_kernel, out_shape=(jax.ShapeDtypeStruct((D, 1024), BF...  10 us
    ppermute x1, waiting for transfers between devices, program(): diag = lax.ppermute(diag, ALL, shift_both(1))  8.36 us
    ppermute x1, starting transfers between devices, program(): diag = lax.ppermute(diag, ALL, shift_both(-1))  8.18 us
    ppermute x6, waiting for transfers between devices, shift_x(): return lax.ppermute(value, ('xl', 'xh'), pairs)  7.93 us
    ppermute x6, starting transfers between devices, shift_x(): return lax.ppermute(value, ('xl', 'xh'), pairs)  7.08 us
    pallas_call x2, Pallas kernels, early_call(): pl.pallas_call(functools.partial(early_kernel, w), out_shape=(wide, wide,...  6.65 us
    ppermute x6, starting transfers between devices, shift_y(): return lax.ppermute(value, 'y', shift(4, k))  5.63 us
  transfers between devices with their start and end apart: 19, of which 7 were waited for; matrix products, arithmetic and copies ran while one was open for 0% of the time, Pallas kernels for 14%

commit v1 on v0

--- a/solution.py
+++ b/solution.py
@@ -322,7 +322,9 @@
             own_ref[lev, r - 9] = dst[at : at + NC, :].astype(BF)
 
 
-def input_high_kernel(gact_ref, xw_ref, dyw_ref, gain_ref, wq_ref, lon0_ref, gg0_ref, own_ref, lon_ref, gg_ref, win, dst):
+def input_high_kernel(
+    gact_ref, xw_ref, dyw_ref, gain_ref, wq_ref, lon0_ref, diag_ref, gg0_ref, own_ref, lon_ref, gg_ref, win, dst
+):
     gain = gain_ref[...]
     acc = gg0_ref[...] + sum(input_rows(w, gact_ref, xw_ref, dyw_ref, gain, wq_ref, win) for w in (0, 1))
     for j in range(8):
@@ -332,6 +334,7 @@
     for at, here, size, _ in lon_out_segments(1):
         dst[at - 48 : at - 48 + size, :] = win[here : here + size, :]
     lon_ref[48:128, :] = dst[0:80, :].astype(BF)
+    lon_ref[128:176, :] = diag_ref[...]
     for own, here, size in own_segments():
         if slot(here) < 2:
             dst[own : own + size, :] = win[here : here + size, :]
@@ -365,29 +368,30 @@
     )(gact, xw, dyw, gain, wq)
 
 
-def input_high_call(gact, xw, dyw, gain, wq, lon0, gg0):
+def input_high_call(*operands):
     return pl.pallas_call(
         input_high_kernel,
         out_shape=(
             jax.ShapeDtypeStruct((LEV, 6, NC, D), BF),
-            jax.ShapeDtypeStruct((128, D), BF),
+            jax.ShapeDtypeStruct((176, D), BF),
             jax.ShapeDtypeStruct((8, 128), F32),
         ),
         scratch_shapes=[pltpu.VMEM((ROWS, D), F32), pltpu.VMEM((ROWS, D), F32)],
         compiler_params=params(24),
         cost_estimate=cost(1e9, 9e6),
         name="input_high",
-    )(gact, xw, dyw, gain, wq, lon0, gg0)
-
-
-def join_kernel(high_ref, low_ref, lat_ref, lon_ref, diag_ref, out_ref, src, dst):
+    )(*operands)
+
+
+def join_kernel(high_ref, low_ref, lat_ref, lon_ref, out_ref, src, dst):
     for lev in range(LEV):
         for r in range(3, NR):
             at = (lev * NR + r) * NC
             part = high_ref[lev, r - 3] if r < 9 else low_ref[lev, r - 9]
             dst[at : at + NC, :] = part.astype(F32)
     lon_parts = [*lon_out_segments(0), *lon_out_segments(1)]
-    for halo, segments in ((lat_ref, lat_segments()), (lon_ref, lon_parts), (diag_ref, diag_segments())):
+    corner = [(LATN + here, at, size, own) for here, at, size, own in diag_segments()]
+    for halo, segments in ((lat_ref, [*lat_segments(), *corner]), (lon_ref, lon_parts)):
         count = halo.shape[0]
         src[:count, :] = halo[...].astype(F32)
         for here, _, size, own in segments:
@@ -398,15 +402,15 @@
             out_ref[lev, r] = dst[at : at + NC, :].astype(BF)
 
 
-def join_call(high, low, lat, lon, diag):
+def join_call(high, low, lat, lon):
     return pl.pallas_call(
         join_kernel,
         out_shape=jax.ShapeDtypeStruct((LEV, NR, NC, D), BF),
-        scratch_shapes=[pltpu.VMEM((128, D), F32), pltpu.VMEM((ROWS, D), F32)],
+        scratch_shapes=[pltpu.VMEM((176, D), F32), pltpu.VMEM((ROWS, D), F32)],
         compiler_params=params(12),
         cost_estimate=cost(1e6, 4e6),
         name="join",
-    )(high, low, lat, lon, diag)
+    )(high, low, lat, lon)
 
 
 MSG = 272
@@ -463,7 +467,9 @@
     )(keep, recv, gg)
 
 
-def cross_kernel(owna, a1, a2, a3, ownb, b1, b2, b3, gg_ref, gout, nowna, na1, na2, na3, nownb, nb1, nb2, nb3):
+def cross_kernel(
+    owna, a1, a2, a3, ownb, b1, b2, b3, gg_ref, gout, nowna, na1, na2, na3, nownb, nb1, nb2, nb3
+):
     y = lax.axis_index("y")
     x = x_of()
     gg = gg_ref[...] + take_gain(a1, 256) + take_gain(a2, 256) + take_gain(a3, 256)
@@ -589,6 +595,13 @@
 ALL = LAT + LON
 
 
+def exchange(move, values):
+    out = []
+    for k, v in enumerate(values):
+        out.append(move(v, k + 1))
+    return out
+
+
 def program(x, dy, gain, wq, wp):
     gain2 = gain.reshape(1, D)
     lat, lon, diag = pack(x, dy)
@@ -601,20 +614,20 @@
     keep, send, gact, xw, dyw = main_call(x, dy, lat, lon, diag, gain2, wq, wp, *early)
     recv = lax.ppermute(send, "c", [(0, 1), (1, 0)])
     low, lat, lon0, diag, gg0 = input_low_call(gact, xw, dyw, gain2, wq)
-    high, lon, gg = input_high_call(gact, xw, dyw, gain2, wq, lon0, gg0)
+    high, lon, gg = input_high_call(gact, xw, dyw, gain2, wq, lon0, diag, gg0)
     oa, a1, a2, a3, ob, b1, b2, b3 = split_call(keep, recv, gg)
-    a1, a2, a3 = (shift_y(v, k) for k, v in ((1, a1), (2, a2), (3, a3)))
-    b1, b2, b3 = (shift_x(v, k) for k, v in ((1, b1), (2, b2), (3, b3)))
+    a1, a2, a3 = exchange(shift_y, (a1, a2, a3))
+    b1, b2, b3 = exchange(shift_x, (b1, b2, b3))
+    lon = lax.ppermute(lon, LON, shift(32, 1))
+    gg, oa, a1, a2, a3, ob, b1, b2, b3 = cross_call(oa, a1, a2, a3, ob, b1, b2, b3, gg)
+    a1, a2, a3 = exchange(shift_x, (a1, a2, a3))
+    b1, b2, b3 = exchange(shift_y, (b1, b2, b3))
+    lat = jnp.concatenate([lat, lon[128:176]], 0)
     lat = lax.ppermute(lat, LAT, shift(8, 1))
-    lon = lax.ppermute(lon, LON, shift(32, 1))
-    diag = lax.ppermute(diag, ALL, shift_both(1))
-    gg, oa, a1, a2, a3, ob, b1, b2, b3 = cross_call(oa, a1, a2, a3, ob, b1, b2, b3, gg)
-    a1, a2, a3 = (shift_x(v, k) for k, v in ((1, a1), (2, a2), (3, a3)))
-    b1, b2, b3 = (shift_y(v, k) for k, v in ((1, b1), (2, b2), (3, b3)))
-    grad_in = join_call(high, low, lat, lon, diag)
-    a1, grad_in = lax.optimization_barrier((a1, grad_in))
     blocks = gather_call(oa, a1, a2, a3, ob, b1, b2, b3, gg)
     blocks = lax.all_to_all(blocks, ("z", "c"), 0, 0, tiled=True)
+    lat, blocks = lax.optimization_barrier((lat, blocks))
+    grad_in = join_call(high, low, lat, lon)
     grad_qkv, grad_proj, grad_gain = final_call(blocks)
     return grad_in, grad_qkv, grad_proj.T, grad_gain.reshape(4)
 

time: 98.5 us -> 104 us (1.056)
  blocking collectives: 17.9 us -> 0 us
  starting transfers between devices: 29.7 us -> 44 us
  waiting for transfers between devices: 18.8 us -> 27.2 us
    all_to_all x1 -> x0, blocking collectives: 17.9 us -> none  [program(): blocks = lax.all_to_all(blocks, ('z', 'c'), 0, 0, tiled=True)]
    all_to_all x0 -> x1, starting transfers between devices: none -> 13.5 us  [program(): blocks = lax.all_to_all(blocks, ('z', 'c'), 0, 0, tiled=True)]
    ppermute x6, waiting for transfers between devices: 7.93 us -> 17.6 us  [shift_x(): return lax.ppermute(value, ('xl', 'xh'), pairs)]
    all_to_all x0 -> x1, waiting for transfers between devices: none -> 9.52 us  [program(): blocks = lax.all_to_all(blocks, ('z', 'c'), 0, 0, tiled=True)]
    ppermute x1 -> x0, waiting for transfers between devices: 8.36 us -> none  [program(): diag = lax.ppermute(diag, ALL, shift_both(1))]
    ppermute x6, starting transfers between devices: 5.63 us -> 10.4 us  [shift_y(): return lax.ppermute(value, 'y', shift(4, k))]
    ppermute x6, waiting for transfers between devices: 2.52 us -> 0.02 us  [shift_y(): return lax.ppermute(value, 'y', shift(4, k))]
    ppermute x6, starting transfers between devices: 7.08 us -> 4.81 us  [shift_x(): return lax.ppermute(value, ('xl', 'xh'), pairs)]
  transfers between devices with their start and end apart: 19 -> 19, of which waited for: 7 -> 7; matrix products, arithmetic and copies ran while one was open for 0% -> 0% of each run, Pallas kernels for 14% -> 13%
where the time goes in v1:
time: 104 us
  starting transfers between devices  44 us (42%)
  Pallas kernels  28.6 us (28%)
  waiting for transfers between devices  27.2 us (26%)
  local copies, waits for them, and re-layouts  3.14 us (3%)
    ppermute x6, waiting for transfers between devices, shift_x(): return lax.ppermute(value, ('xl', 'xh'), pairs)  17.6 us
    all_to_all x1, starting transfers between devices, program(): blocks = lax.all_to_all(blocks, ('z', 'c'), 0, 0, tiled=True)  13.5 us
    ppermute x6, starting transfers between devices, shift_y(): return lax.ppermute(value, 'y', shift(4, k))  10.4 us
    pallas_call x1, Pallas kernels, main_call(): pl.pallas_call(main_kernel, out_shape=(jax.ShapeDtypeStruct((D, 1024), BF...  10 us
    all_to_all x1, waiting for transfers between devices, program(): blocks = lax.all_to_all(blocks, ('z', 'c'), 0, 0, tiled=True)  9.52 us
    ppermute x1, starting transfers between devices, program(): diag = lax.ppermute(diag, ALL, shift_both(-1))  8.18 us
    pallas_call x2, Pallas kernels, early_call(): pl.pallas_call(functools.partial(early_kernel, w), out_shape=(wide, wide,...  6.65 us
    ppermute x6, starting transfers between devices, shift_x(): return lax.ppermute(value, ('xl', 'xh'), pairs)  4.81 us
  transfers between devices with their start and end apart: 19, of which 7 were waited for; matrix products, arithmetic and copies ran while one was open for 0% of the time, Pallas kernels for 13%

profile of v1, /device:TPU:1, one launch (start us, length us, event | category | flops | bytes accessed | tf_op | source)
XLA Modules:
  0.0 103.8 jit_solution(4022548677564108517)
XLA Ops:
  0.7 2.7 %pack.1 = (bf16[2,112,1024]{2,1,0:T(8,128)(2,1)}, bf16[2,112,1024]{2,1,0:T(8,128)(2,1)}, bf16[2,48,1024]{2,1,0:T(8,128)(2,1)}) custom-call(bf16[2,12,24,1024]{3,2,1,0:T(8,128)(2,1)} %x_ref.7, bf16[2,12,24,1024]{3,2,1,0:T(8,128)(2,1)} %dy_ref.7), custom_call_target="tpu_custom_call" | custom-call | flops 1000000 | bytes 4000000 | tf_op jit(solution)/shard_map/pack/pallas_call | solution.py:106
  3.4 3.3 %collective-permute-start.1 = (bf16[2,112,1024]{2,1,0:T(8,128)(2,1)}, bf16[2,112,1024]{2,1,0:T(8,128)(2,1)S(1)}, u32[]{:S(2)}, u32[]{:S(2)}) collective-permute-start(bf16[2,112,1024]{2,1,0:T(8,128)(2,1)} %get-tuple-element.53), channel_id=1, source_target_pairs={{0,31},{1,0},{2,1},{3,2},{4,3},{5,4},{6,5},{7,6},{8,7},{9,8},{10,9... | collective-permute-start | bytes 1376264 | tf_op jit(solution)/shard_map/ppermute | solution.py:608
  6.6 2.0 %collective-permute-start = (bf16[2,112,1024]{2,1,0:T(8,128)(2,1)}, bf16[2,112,1024]{2,1,0:T(8,128)(2,1)S(1)}, u32[]{:S(2)}, u32[]{:S(2)}) collective-permute-start(bf16[2,112,1024]{2,1,0:T(8,128)(2,1)} %get-tuple-element.52), channel_id=1, source_target_pairs={{0,224},{32,0},{64,32},{96,64},{128,96},{160,128},{192,160},{224,1... | collective-permute-start | bytes 1376264 | tf_op jit(solution)/shard_map/ppermute | solution.py:609
  8.6 8.2 %collective-permute-start.2 = (bf16[2,48,1024]{2,1,0:T(8,128)(2,1)}, bf16[2,48,1024]{2,1,0:T(8,128)(2,1)S(1)}, u32[]{:S(2)}, u32[]{:S(2)}) collective-permute-start(bf16[2,48,1024]{2,1,0:T(8,128)(2,1)} %get-tuple-element.56), channel_id=1, source_target_pairs={{0,255},{1,224},{2,225},{3,226},{4,227},{5,228},{6,229},{7,230},{8... | collective-permute-start | bytes 589832 | tf_op jit(solution)/shard_map/ppermute | solution.py:610
  16.8 1.9 %copy-done = bf16[1024,1536]{1,0:T(8,128)(2,1)S(1)} copy-done((bf16[1024,1536]{1,0:T(8,128)(2,1)S(1)}, bf16[1024,1536]{1,0:T(8,128)(2,1)}, u32[]{:S(2)}) %copy-start) | copy-done | bytes 3145752
  18.7 1.2 %copy-done.5 = bf16[512,1024]{1,0:T(8,128)(2,1)S(1)} copy-done((bf16[512,1024]{1,0:T(8,128)(2,1)S(1)}, bf16[512,1024]{1,0:T(8,128)(2,1)}, u32[]{:S(2)}) %copy-start.5) | copy-done | bytes 1048600
  19.9 3.3 %shard_map.84 = (bf16[144,1024]{1,0:T(8,128)(2,1)S(1)}, bf16[144,1024]{1,0:T(8,128)(2,1)S(1)}, bf16[144,1024]{1,0:T(8,128)(2,1)S(1)}, bf16[144,2048]{1,0:T(8,128)(2,1)S(1)}) custom-call(bf16[2,12,24,1024]{3,2,1,0:T(8,128)(2,1)S(1)} %copy-done.2, bf16[2,12,24,1024]{3,2,1,0:T(8,128)(2,1)S(1)} %copy-done.3, f32[1,1024]{1,0:T(1,128)S(1)} %bitcast.3, ...), custom_call_target="tpu_custom_call" | custom-call | flops 2000000000 | bytes 9000000 | tf_op jit(solution)/shard_map/pallas_call | solution.py:221
  23.2 0.0 collective-permute-done.1.refs_0_.lon_ref
  23.3 0.0 copy-start.1
  23.3 0.0 copy-start.6
  23.3 3.3 %shard_map.85 = (bf16[144,1024]{1,0:T(8,128)(2,1)S(1)}, bf16[144,1024]{1,0:T(8,128)(2,1)S(1)}, bf16[144,1024]{1,0:T(8,128)(2,1)S(1)}, bf16[144,2048]{1,0:T(8,128)(2,1)S(1)}) custom-call(bf16[2,12,24,1024]{3,2,1,0:T(8,128)(2,1)S(1)} %copy-done.2, bf16[2,12,24,1024]{3,2,1,0:T(8,128)(2,1)S(1)} %copy-done.3, ...), custom_call_target="tpu_custom_call" | custom-call | flops 2000000000 | bytes 9000000 | tf_op jit(solution)/shard_map/pallas_call | solution.py:221
  26.6 0.0 collective-permute-done.2.diag_ref
  26.6 0.0 collective-permute-done.lat_ref
  26.6 10.0 %main.1 = (bf16[1024,1024]{1,0:T(8,128)(2,1)S(1)}, bf16[1024,1024]{1,0:T(8,128)(2,1)S(1)}, bf16[576,2048]{1,0:T(8,128)(2,1)S(1)}, bf16[576,1024]{1,0:T(8,128)(2,1)S(1)}, bf16[576,1024]{1,0:T(8,128)(2,1)S(1)}) custom-call(bf16[2,12,24,1024]{3,2,1,0:T(8,128)(2,1)S(1)} %copy-done.2, bf16[2,12,24,1024]{3,2,1,0:T(8,128)(2,1)S(1)} %copy-done.3, ...), custom_call_target="tpu_custom_call" | custom-call | flops 5500000256 | bytes 14000000 | tf_op jit(solution)/shard_map/main/pallas_call | solution.py:270
  36.6 0.1 collective-permute-start.5
  36.7 2.8 %input_low.1 = (bf16[2,3,24,1024]{3,2,1,0:T(8,128)(2,1)S(1)}, bf16[112,1024]{1,0:T(8,128)(2,1)S(1)}, bf16[48,1024]{1,0:T(8,128)(2,1)S(1)}, bf16[48,1024]{1,0:T(8,128)(2,1)S(1)}, f32[1,1024]{1,0:T(1,128)S(1)}) custom-call(bf16[576,2048]{1,0:T(8,128)(2,1)S(1)} %get-tuple-element.65.gact_ref, bf16[576,1024]{1,0:T(8,128)(2,1)S(1)} %get-tuple-element.66.xw_ref, ...), custom_call_target="tpu_custom_call" | custom-call | flops 1000000000 | bytes 9000000 | tf_op jit(solution)/shard_map/input_low/pallas_call | solution.py:355
  39.5 2.8 %input_high.1 = (bf16[2,6,24,1024]{3,2,1,0:T(8,128)(2,1)S(1)}, bf16[176,1024]{1,0:T(8,128)(2,1)S(1)}, f32[8,128]{1,0:T(8,128)S(1)}) custom-call(bf16[576,2048]{1,0:T(8,128)(2,1)S(1)} %get-tuple-element.65.gact_ref, bf16[576,1024]{1,0:T(8,128)(2,1)S(1)} %get-tuple-element.66.xw_ref, bf16[576,1024]{1,0:T(8,128)(2,1)S(1)} %get-tuple-element.67.dyw_ref, ...), custom_call_target="tpu_custom_call" | custom-call | flops 1000000000 | bytes 9000000 | tf_op jit(solution)/shard_map/input_high/pallas_call | solution.py:372
  42.4 0.0 collective-permute-done.5.recv_ref
  42.4 0.5 split.1
  42.9 0.4 collective-permute-start.9
  43.3 1.7 %collective-permute-start.10 = (bf16[256,512]{1,0:T(8,128)(2,1)S(1)}, bf16[256,512]{1,0:T(8,128)(2,1)S(1)}, u32[]{:S(2)}, u32[]{:S(2)}) collective-permute-start(bf16[256,512]{1,0:T(8,128)(2,1)S(1)} %get-tuple-element.84), channel_id=1, source_target_pairs={{0,16},{16,0},{32,48},{48,32},{1,17},{17,1},{33,49},{49,33},{2,18}... | collective-permute-start | bytes 786440 | tf_op jit(solution)/shard_map/ppermute | solution.py:574
  45.0 0.3 collective-permute-start.3
  45.3 1.3 %collective-permute-start.6 = (bf16[272,512]{1,0:T(8,128)(2,1)S(1)}, bf16[272,512]{1,0:T(8,128)(2,1)S(1)}, u32[]{:S(2)}, u32[]{:S(2)}) collective-permute-start(bf16[272,512]{1,0:T(8,128)(2,1)S(1)} %get-tuple-element.79), channel_id=1, source_target_pairs={{0,64},{64,128},{128,192},{192,0},{1,65},{65,129},{129,193},{193,1... | collective-permute-start | bytes 835592 | tf_op jit(solution)/shard_map/ppermute | solution.py:578
  46.6 3.8 %collective-permute-start.7 = (bf16[272,512]{1,0:T(8,128)(2,1)S(1)}, bf16[272,512]{1,0:T(8,128)(2,1)S(1)}, u32[]{:S(2)}, u32[]{:S(2)}) collective-permute-start(bf16[272,512]{1,0:T(8,128)(2,1)S(1)} %get-tuple-element.80), channel_id=1, source_target_pairs={{0,128},{64,192},{128,0},{192,64},{1,129},{65,193},{129,1},{193,65... | collective-permute-start | bytes 835592 | tf_op jit(solution)/shard_map/ppermute | solution.py:578
  50.4 1.7 %collective-permute-done.9.b1 = bf16[256,512]{1,0:T(8,128)(2,1)S(1)} collective-permute-done((bf16[256,512]{1,0:T(8,128)(2,1)S(1)}, bf16[256,512]{1,0:T(8,128)(2,1)S(1)}, u32[]{:S(2)}, u32[]{:S(2)}) %collective-permute-start.9) | collective-permute-done | bytes 262176 | tf_op jit(solution)/shard_map/ppermute | solution.py:574
  52.2 8.3 %collective-permute-done.10.b2 = bf16[256,512]{1,0:T(8,128)(2,1)S(1)} collective-permute-done((bf16[256,512]{1,0:T(8,128)(2,1)S(1)}, bf16[256,512]{1,0:T(8,128)(2,1)S(1)}, u32[]{:S(2)}, u32[]{:S(2)}) %collective-permute-start.10) | collective-permute-done | bytes 262176 | tf_op jit(solution)/shard_map/ppermute | solution.py:574
  60.4 0.0 collective-permute-start.11
  60.4 5.9 %collective-permute-done.11.b3 = bf16[256,512]{1,0:T(8,128)(2,1)S(1)} collective-permute-done((bf16[256,512]{1,0:T(8,128)(2,1)S(1)}, bf16[256,512]{1,0:T(8,128)(2,1)S(1)}, u32[]{:S(2)}, u32[]{:S(2)}) %collective-permute-start.11) | collective-permute-done | bytes 262176 | tf_op jit(solution)/shard_map/ppermute | solution.py:574
  66.3 0.0 collective-permute-done.6.a1
  66.3 0.0 collective-permute-done.7.a2
  66.3 0.3 cross.1
  66.6 0.1 collective-permute-start.15
  66.7 4.9 %collective-permute-start.16 = (bf16[64,512]{1,0:T(8,128)(2,1)S(1)}, bf16[64,512]{1,0:T(8,128)(2,1)S(1)}, u32[]{:S(2)}, u32[]{:S(2)}) collective-permute-start(bf16[64,512]{1,0:T(8,128)(2,1)S(1)} %get-tuple-element.92), channel_id=1, source_target_pairs={{0,128},{64,192},{128,0},{192,64},{1,129},{65,193},{129,1},{193,65... | collective-permute-start | bytes 196616 | tf_op jit(solution)/shard_map/ppermute | solution.py:578
  71.6 0.3 collective-permute-start.17
  71.9 0.0 collective-permute-start.12
  71.9 2.7 %collective-permute-start.13 = (bf16[80,512]{1,0:T(8,128)(2,1)S(1)}, bf16[80,512]{1,0:T(8,128)(2,1)S(1)}, u32[]{:S(2)}, u32[]{:S(2)}) collective-permute-start(bf16[80,512]{1,0:T(8,128)(2,1)S(1)} %get-tuple-element.88), channel_id=1, source_target_pairs={{0,16},{16,0},{32,48},{48,32},{1,17},{17,1},{33,49},{49,33},{2,18}... | collective-permute-start | bytes 245768 | tf_op jit(solution)/shard_map/ppermute | solution.py:574
  74.6 0.0 collective-permute-done.15.b1
  74.6 0.0 collective-permute-start.14
  74.6 0.0 collective-permute-done.16.b2
  74.6 1.5 %collective-permute-start.4 = (bf16[160,1024]{1,0:T(8,128)(2,1)S(1)}, bf16[160,1024]{1,0:T(8,128)(2,1)S(1)}, u32[]{:S(2)}, u32[]{:S(2)}) collective-permute-start(bf16[160,1024]{1,0:T(8,128)(2,1)S(1)} %pad_maximum_fusion), channel_id=1, source_target_pairs={{0,32},{32,64},{64,96},{96,128},{128,160},{160,192},{192,224},{224... | collective-permute-start | bytes 983048 | tf_op jit(solution)/shard_map/ppermute | solution.py:626
  76.2 0.4 collective-permute-done.12.a1
  76.6 0.7 collective-permute-done.13.a2
  77.3 0.6 collective-permute-done.14.a3
  77.9 0.7 gather.1
  78.6 13.5 %all-to-all-start = ((bf16[16,8,640]{2,1,0:T(8,128)(2,1)}), bf16[16,8,640]{2,1,0:T(8,128)(2,1)S(1)}, u32[]{:S(2)}, u32[]{:S(2)}) async-start(bf16[16,8,640]{2,1,0:T(8,128)(2,1)} %gather.1), calls=%async_computation | async-start | bytes 327680 | tf_op jit(solution)/shard_map/all_to_all | solution.py:628
  92.1 9.5 %all-to-all-done.blocks = bf16[16,8,640]{2,1,0:T(8,128)(2,1)S(1)} async-done(((bf16[16,8,640]{2,1,0:T(8,128)(2,1)}), bf16[16,8,640]{2,1,0:T(8,128)(2,1)S(1)}, u32[]{:S(2)}, u32[]{:S(2)}) %all-to-all-start) | async-done | bytes 163872 | tf_op jit(solution)/shard_map/all_to_all | solution.py:628
  101.7 0.6 final.1
  102.3 1.5 %join.1 = bf16[2,12,24,1024]{3,2,1,0:T(8,128)(2,1)} custom-call(bf16[2,6,24,1024]{3,2,1,0:T(8,128)(2,1)S(1)} %get-tuple-element.71.high_ref, bf16[2,3,24,1024]{3,2,1,0:T(8,128)(2,1)S(1)} %get-tuple-element.72.low_ref, bf16[160,1024]{1,0:T(8,128)(2,1)S(1)} %collective-permute-done.4.lat_ref, bf16[176,1024]{1,0:T(8,128)(2,1)S(1)} %collective-permute-done.3.lon_ref), custom_call_target="tpu_custom_call" | custom-call | flops 1000000 | bytes 4000000 | tf_op jit(solution)/shard_map/join/pallas_call | solution.py:406
  (17 shorter events, 0.1 us)
Async XLA Ops:
  0.6 16.1 %copy-start.3 = (bf16[2,12,24,1024]{3,2,1,0:T(8,128)(2,1)S(1)}, bf16[2,12,24,1024]{3,2,1,0:T(8,128)(2,1)}, u32[]{:S(2)}) copy-start(bf16[2,12,24,1024]{3,2,1,0:T(8,128)(2,1)} %dy_ref.7) | copy-start | bytes 3538948
  0.6 16.1 %copy-start.2 = (bf16[2,12,24,1024]{3,2,1,0:T(8,128)(2,1)S(1)}, bf16[2,12,24,1024]{3,2,1,0:T(8,128)(2,1)}, u32[]{:S(2)}) copy-start(bf16[2,12,24,1024]{3,2,1,0:T(8,128)(2,1)} %x_ref.7) | copy-start | bytes 3538948
  0.7 16.1 %copy-start.4 = (f32[1024]{0:T(1024)S(1)}, f32[1024]{0:T(1024)}, u32[]{:S(2)}) copy-start(f32[1024]{0:T(1024)} %param.7) | copy-start | bytes 12292
  3.4 19.9 %collective-permute-start.1 = (bf16[2,112,1024]{2,1,0:T(8,128)(2,1)}, bf16[2,112,1024]{2,1,0:T(8,128)(2,1)S(1)}, u32[]{:S(2)}, u32[]{:S(2)}) collective-permute-start(bf16[2,112,1024]{2,1,0:T(8,128)(2,1)} %get-tuple-element.53), channel_id=1, source_target_pairs={{0,31},{1,0},{2,1},{3,2},{4,3},{5,4},{6,5},{7,6},{8,7},{9,8},{10,9... | collective-permute-start | bytes 1376264 | tf_op jit(solution)/shard_map/ppermute | solution.py:608
  6.6 20.0 %collective-permute-start = (bf16[2,112,1024]{2,1,0:T(8,128)(2,1)}, bf16[2,112,1024]{2,1,0:T(8,128)(2,1)S(1)}, u32[]{:S(2)}, u32[]{:S(2)}) collective-permute-start(bf16[2,112,1024]{2,1,0:T(8,128)(2,1)} %get-tuple-element.52), channel_id=1, source_target_pairs={{0,224},{32,0},{64,32},{96,64},{128,96},{160,128},{192,160},{224,1... | collective-permute-start | bytes 1376264 | tf_op jit(solution)/shard_map/ppermute | solution.py:609
  8.6 18.0 %collective-permute-start.2 = (bf16[2,48,1024]{2,1,0:T(8,128)(2,1)}, bf16[2,48,1024]{2,1,0:T(8,128)(2,1)S(1)}, u32[]{:S(2)}, u32[]{:S(2)}) collective-permute-start(bf16[2,48,1024]{2,1,0:T(8,128)(2,1)} %get-tuple-element.56), channel_id=1, source_target_pairs={{0,255},{1,224},{2,225},{3,226},{4,227},{5,228},{6,229},{7,230},{8... | collective-permute-start | bytes 589832 | tf_op jit(solution)/shard_map/ppermute | solution.py:610
  16.8 1.9 %copy-start = (bf16[1024,1536]{1,0:T(8,128)(2,1)S(1)}, bf16[1024,1536]{1,0:T(8,128)(2,1)}, u32[]{:S(2)}) copy-start(bf16[1024,1536]{1,0:T(8,128)(2,1)} %wq_ref.5) | copy-start | bytes 9437188
  18.7 1.2 %copy-start.5 = (bf16[512,1024]{1,0:T(8,128)(2,1)S(1)}, bf16[512,1024]{1,0:T(8,128)(2,1)}, u32[]{:S(2)}) copy-start(bf16[512,1024]{1,0:T(8,128)(2,1)} %wp_ref.1) | copy-start | bytes 3145732
  23.3 3.4 %copy-start.1 = (bf16[1024,1536]{1,0:T(8,128)(2,1)S(1)}, bf16[1024,1536]{1,0:T(8,128)(2,1)}, u32[]{:S(2)}) copy-start(bf16[1024,1536]{1,0:T(8,128)(2,1)} %wq_ref.5) | copy-start | bytes 9437188
  23.3 3.4 %copy-start.6 = (bf16[512,1024]{1,0:T(8,128)(2,1)S(1)}, bf16[512,1024]{1,0:T(8,128)(2,1)}, u32[]{:S(2)}) copy-start(bf16[512,1024]{1,0:T(8,128)(2,1)} %wp_ref.1) | copy-start | bytes 3145732
  36.6 5.7 %collective-permute-start.5 = (bf16[1024,1024]{1,0:T(8,128)(2,1)S(1)}, bf16[1024,1024]{1,0:T(8,128)(2,1)S(1)}, u32[]{:S(2)}, u32[]{:S(2)}) collective-permute-start(bf16[1024,1024]{1,0:T(8,128)(2,1)S(1)} %get-tuple-element.76), channel_id=1, source_target_pairs={{0,1},{1,0},{2,3},{3,2},{4,5},{5,4},{6,7},{7,6},{8,9},{9,8},{10,11... | collective-permute-start | bytes 6291464 | tf_op jit(solution)/shard_map/ppermute | solution.py:615
  42.9 9.3 %collective-permute-start.9 = (bf16[256,512]{1,0:T(8,128)(2,1)S(1)}, bf16[256,512]{1,0:T(8,128)(2,1)S(1)}, u32[]{:S(2)}, u32[]{:S(2)}) collective-permute-start(bf16[256,512]{1,0:T(8,128)(2,1)S(1)} %get-tuple-element.83), channel_id=1, source_target_pairs={{0,32},{16,48},{32,16},{48,0},{1,33},{17,49},{33,17},{49,1},{2,34}... | collective-permute-start | bytes 786440 | tf_op jit(solution)/shard_map/ppermute | solution.py:574
  43.3 17.2 %collective-permute-start.10 = (bf16[256,512]{1,0:T(8,128)(2,1)S(1)}, bf16[256,512]{1,0:T(8,128)(2,1)S(1)}, u32[]{:S(2)}, u32[]{:S(2)}) collective-permute-start(bf16[256,512]{1,0:T(8,128)(2,1)S(1)} %get-tuple-element.84), channel_id=1, source_target_pairs={{0,16},{16,0},{32,48},{48,32},{1,17},{17,1},{33,49},{49,33},{2,18}... | collective-permute-start | bytes 786440 | tf_op jit(solution)/shard_map/ppermute | solution.py:574
  45.0 21.7 %collective-permute-start.3 = (bf16[176,1024]{1,0:T(8,128)(2,1)S(1)}, bf16[176,1024]{1,0:T(8,128)(2,1)S(1)}, u32[]{:S(2)}, u32[]{:S(2)}) collective-permute-start(bf16[176,1024]{1,0:T(8,128)(2,1)S(1)} %get-tuple-element.74), channel_id=1, source_target_pairs={{0,1},{1,2},{2,3},{3,4},{4,5},{5,6},{6,7},{7,8},{8,9},{9,10},{10,1... | collective-permute-start | bytes 1081352 | tf_op jit(solution)/shard_map/ppermute | solution.py:621
  45.3 21.1 %collective-permute-start.6 = (bf16[272,512]{1,0:T(8,128)(2,1)S(1)}, bf16[272,512]{1,0:T(8,128)(2,1)S(1)}, u32[]{:S(2)}, u32[]{:S(2)}) collective-permute-start(bf16[272,512]{1,0:T(8,128)(2,1)S(1)} %get-tuple-element.79), channel_id=1, source_target_pairs={{0,64},{64,128},{128,192},{192,0},{1,65},{65,129},{129,193},{193,1... | collective-permute-start | bytes 835592 | tf_op jit(solution)/shard_map/ppermute | solution.py:578
  46.6 19.8 %collective-permute-start.7 = (bf16[272,512]{1,0:T(8,128)(2,1)S(1)}, bf16[272,512]{1,0:T(8,128)(2,1)S(1)}, u32[]{:S(2)}, u32[]{:S(2)}) collective-permute-start(bf16[272,512]{1,0:T(8,128)(2,1)S(1)} %get-tuple-element.80), channel_id=1, source_target_pairs={{0,128},{64,192},{128,0},{192,64},{1,129},{65,193},{129,1},{193,65... | collective-permute-start | bytes 835592 | tf_op jit(solution)/shard_map/ppermute | solution.py:578
  52.2 14.2 %collective-permute-start.8 = (bf16[272,512]{1,0:T(8,128)(2,1)S(1)}, bf16[272,512]{1,0:T(8,128)(2,1)S(1)}, u32[]{:S(2)}, u32[]{:S(2)}) collective-permute-start(bf16[272,512]{1,0:T(8,128)(2,1)S(1)} %get-tuple-element.81), channel_id=1, source_target_pairs={{0,192},{64,0},{128,64},{192,128},{1,193},{65,1},{129,65},{193,129... | collective-permute-start | bytes 835592 | tf_op jit(solution)/shard_map/ppermute | solution.py:578
  60.4 5.9 %collective-permute-start.11 = (bf16[256,512]{1,0:T(8,128)(2,1)S(1)}, bf16[256,512]{1,0:T(8,128)(2,1)S(1)}, u32[]{:S(2)}, u32[]{:S(2)}) collective-permute-start(bf16[256,512]{1,0:T(8,128)(2,1)S(1)} %get-tuple-element.85), channel_id=1, source_target_pairs={{0,48},{16,32},{32,0},{48,16},{1,49},{17,33},{33,1},{49,17},{2,50}... | collective-permute-start | bytes 786440 | tf_op jit(solution)/shard_map/ppermute | solution.py:574
  66.6 8.0 %collective-permute-start.15 = (bf16[64,512]{1,0:T(8,128)(2,1)S(1)}, bf16[64,512]{1,0:T(8,128)(2,1)S(1)}, u32[]{:S(2)}, u32[]{:S(2)}) collective-permute-start(bf16[64,512]{1,0:T(8,128)(2,1)S(1)} %get-tuple-element.91), channel_id=1, source_target_pairs={{0,64},{64,128},{128,192},{192,0},{1,65},{65,129},{129,193},{193,1... | collective-permute-start | bytes 196616 | tf_op jit(solution)/shard_map/ppermute | solution.py:578
  66.7 7.9 %collective-permute-start.16 = (bf16[64,512]{1,0:T(8,128)(2,1)S(1)}, bf16[64,512]{1,0:T(8,128)(2,1)S(1)}, u32[]{:S(2)}, u32[]{:S(2)}) collective-permute-start(bf16[64,512]{1,0:T(8,128)(2,1)S(1)} %get-tuple-element.92), channel_id=1, source_target_pairs={{0,128},{64,192},{128,0},{192,64},{1,129},{65,193},{129,1},{193,65... | collective-permute-start | bytes 196616 | tf_op jit(solution)/shard_map/ppermute | solution.py:578
  71.6 4.6 %collective-permute-start.17 = (bf16[64,512]{1,0:T(8,128)(2,1)S(1)}, bf16[64,512]{1,0:T(8,128)(2,1)S(1)}, u32[]{:S(2)}, u32[]{:S(2)}) collective-permute-start(bf16[64,512]{1,0:T(8,128)(2,1)S(1)} %get-tuple-element.93), channel_id=1, source_target_pairs={{0,192},{64,0},{128,64},{192,128},{1,193},{65,1},{129,65},{193,129... | collective-permute-start | bytes 196616 | tf_op jit(solution)/shard_map/ppermute | solution.py:578
  71.9 4.7 %collective-permute-start.12 = (bf16[80,512]{1,0:T(8,128)(2,1)S(1)}, bf16[80,512]{1,0:T(8,128)(2,1)S(1)}, u32[]{:S(2)}, u32[]{:S(2)}) collective-permute-start(bf16[80,512]{1,0:T(8,128)(2,1)S(1)} %get-tuple-element.87), channel_id=1, source_target_pairs={{0,32},{16,48},{32,16},{48,0},{1,33},{17,49},{33,17},{49,1},{2,34}... | collective-permute-start | bytes 245768 | tf_op jit(solution)/shard_map/ppermute | solution.py:574
  71.9 5.4 %collective-permute-start.13 = (bf16[80,512]{1,0:T(8,128)(2,1)S(1)}, bf16[80,512]{1,0:T(8,128)(2,1)S(1)}, u32[]{:S(2)}, u32[]{:S(2)}) collective-permute-start(bf16[80,512]{1,0:T(8,128)(2,1)S(1)} %get-tuple-element.88), channel_id=1, source_target_pairs={{0,16},{16,0},{32,48},{48,32},{1,17},{17,1},{33,49},{49,33},{2,18}... | collective-permute-start | bytes 245768 | tf_op jit(solution)/shard_map/ppermute | solution.py:574
  74.6 3.3 %collective-permute-start.14 = (bf16[80,512]{1,0:T(8,128)(2,1)S(1)}, bf16[80,512]{1,0:T(8,128)(2,1)S(1)}, u32[]{:S(2)}, u32[]{:S(2)}) collective-permute-start(bf16[80,512]{1,0:T(8,128)(2,1)S(1)} %get-tuple-element.89), channel_id=1, source_target_pairs={{0,48},{16,32},{32,0},{48,16},{1,49},{17,33},{33,1},{49,17},{2,50}... | collective-permute-start | bytes 245768 | tf_op jit(solution)/shard_map/ppermute | solution.py:574
  74.6 17.5 %collective-permute-start.4 = (bf16[160,1024]{1,0:T(8,128)(2,1)S(1)}, bf16[160,1024]{1,0:T(8,128)(2,1)S(1)}, u32[]{:S(2)}, u32[]{:S(2)}) collective-permute-start(bf16[160,1024]{1,0:T(8,128)(2,1)S(1)} %pad_maximum_fusion), channel_id=1, source_target_pairs={{0,32},{32,64},{64,96},{96,128},{128,160},{160,192},{192,224},{224... | collective-permute-start | bytes 983048 | tf_op jit(solution)/shard_map/ppermute | solution.py:626
  78.6 23.0 %all-to-all-start = ((bf16[16,8,640]{2,1,0:T(8,128)(2,1)}), bf16[16,8,640]{2,1,0:T(8,128)(2,1)S(1)}, u32[]{:S(2)}, u32[]{:S(2)}) async-start(bf16[16,8,640]{2,1,0:T(8,128)(2,1)} %gather.1), calls=%async_computation | async-start | bytes 327680 | tf_op jit(solution)/shard_map/all_to_all | solution.py:628

commit v2 on v1

--- a/solution.py
+++ b/solution.py
@@ -31,8 +31,8 @@
     return lax.dot_general(a, b, dims, preferred_element_type=F32)
 
 
-def params(mib):
-    return pltpu.CompilerParams(vmem_limit_bytes=mib * 1024 * 1024)
+def params(mib, **more):
+    return pltpu.CompilerParams(vmem_limit_bytes=mib * 1024 * 1024, **more)
 
 
 def cost(flops, nbytes):
@@ -383,34 +383,68 @@
     )(*operands)
 
 
-def join_kernel(high_ref, low_ref, lat_ref, lon_ref, out_ref, src, dst):
-    for lev in range(LEV):
-        for r in range(3, NR):
-            at = (lev * NR + r) * NC
-            part = high_ref[lev, r - 3] if r < 9 else low_ref[lev, r - 9]
-            dst[at : at + NC, :] = part.astype(F32)
-    lon_parts = [*lon_out_segments(0), *lon_out_segments(1)]
+def join_rest_kernel(high_ref, low_ref, lon_ref, out_ref, src, dst):
+    step = pl.program_id(0)
+
+    @pl.when(step == 0)
+    def _():
+        for lev in range(LEV):
+            for r in range(3, NR):
+                at = (lev * NR + r) * NC
+                part = high_ref[lev, r - 3] if r < 9 else low_ref[lev, r - 9]
+                dst[at : at + NC, :] = part.astype(F32)
+        src[0:128, :] = lon_ref[0:128, :].astype(F32)
+        for here, _, size, own in [*lon_out_segments(0), *lon_out_segments(1)]:
+            dst[own : own + size, :] = src[here : here + size, :]
+
+    for lev in range(LEV):
+        for r in range(3):
+            at = pl.multiple_of((lev * NR + 3 + r + 3 * step) * NC, 8)
+            out_ref[lev, r] = dst[pl.ds(at, NC), :].astype(BF)
+
+
+def join_top_kernel(lat_ref, rest_ref, out_ref, src, dst):
+    src[...] = lat_ref[...].astype(F32)
     corner = [(LATN + here, at, size, own) for here, at, size, own in diag_segments()]
-    for halo, segments in ((lat_ref, [*lat_segments(), *corner]), (lon_ref, lon_parts)):
-        count = halo.shape[0]
-        src[:count, :] = halo[...].astype(F32)
-        for here, _, size, own in segments:
-            dst[own : own + size, :] = src[here : here + size, :]
-    for lev in range(LEV):
-        for r in range(NR):
+    for here, _, size, own in [*lat_segments(), *corner]:
+        dst[own : own + size, :] = src[here : here + size, :]
+    for lev in range(LEV):
+        for r in range(3):
             at = (lev * NR + r) * NC
             out_ref[lev, r] = dst[at : at + NC, :].astype(BF)
 
 
-def join_call(high, low, lat, lon):
-    return pl.pallas_call(
-        join_kernel,
-        out_shape=jax.ShapeDtypeStruct((LEV, NR, NC, D), BF),
-        scratch_shapes=[pltpu.VMEM((176, D), F32), pltpu.VMEM((ROWS, D), F32)],
+WHOLE = pl.BlockSpec(memory_space=pltpu.VMEM)
+GRID_OUT = jax.ShapeDtypeStruct((LEV, NR, NC, D), BF)
+
+
+def join_rest(high, low, lon):
+    return pl.pallas_call(
+        join_rest_kernel,
+        grid=(3,),
+        in_specs=[WHOLE] * 3,
+        out_specs=pl.BlockSpec((LEV, 3, NC, D), lambda i: (0, i + 1, 0, 0)),
+        out_shape=GRID_OUT,
+        scratch_shapes=[pltpu.VMEM((128, D), F32), pltpu.VMEM((ROWS, D), F32)],
         compiler_params=params(12),
         cost_estimate=cost(1e6, 4e6),
-        name="join",
-    )(high, low, lat, lon)
+        name="join_rest",
+    )(high, low, lon)
+
+
+def join_top(lat, rest):
+    return pl.pallas_call(
+        join_top_kernel,
+        grid=(1,),
+        in_specs=[WHOLE, pl.BlockSpec(memory_space=pl.ANY)],
+        out_specs=pl.BlockSpec((LEV, 3, NC, D), lambda i: (0, 0, 0, 0)),
+        out_shape=GRID_OUT,
+        input_output_aliases={1: 0},
+        scratch_shapes=[pltpu.VMEM((160, D), F32), pltpu.VMEM((ROWS, D), F32)],
+        compiler_params=params(8),
+        cost_estimate=cost(1e6, 2e6),
+        name="join_top",
+    )(lat, rest)
 
 
 MSG = 272
@@ -624,10 +658,12 @@
     b1, b2, b3 = exchange(shift_y, (b1, b2, b3))
     lat = jnp.concatenate([lat, lon[128:176]], 0)
     lat = lax.ppermute(lat, LAT, shift(8, 1))
+    rest = join_rest(high, low, lon)
+    a1, rest = lax.optimization_barrier((a1, rest))
     blocks = gather_call(oa, a1, a2, a3, ob, b1, b2, b3, gg)
     blocks = lax.all_to_all(blocks, ("z", "c"), 0, 0, tiled=True)
     lat, blocks = lax.optimization_barrier((lat, blocks))
-    grad_in = join_call(high, low, lat, lon)
+    grad_in = join_top(lat, rest)
     grad_qkv, grad_proj, grad_gain = final_call(blocks)
     return grad_in, grad_qkv, grad_proj.T, grad_gain.reshape(4)
 

time: 104 us -> 103 us (level)
  starting transfers between devices: 44 us -> 42 us
  Pallas kernels: 28.6 us -> 29.7 us
    ppermute x1, starting transfers between devices: 1.54 us -> 0.01 us  [program(): lat = lax.ppermute(lat, LAT, shift(8, 1))]
    pallas_call x1 -> x2, Pallas kernels: 1.47 us -> 2.58 us  [the longest x1 1.71 us: join_rest(): pl.pallas_call(join_rest_kernel, grid=(3,), in_specs=[WHOLE] * 3, out_spe...]
  transfers between devices with their start and end apart: 19 -> 19, of which waited for: 7 -> 5; matrix products, arithmetic and copies ran while one was open for 0% -> 0% of each run, Pallas kernels for 13% -> 15%
where the time goes in v2:
time: 103 us
  starting transfers between devices  42 us (41%)
  Pallas kernels  29.7 us (29%)
  waiting for transfers between devices  27.5 us (27%)
  local copies, waits for them, and re-layouts  3.14 us (3%)
    ppermute x6, waiting for transfers between devices, shift_x(): return lax.ppermute(value, ('xl', 'xh'), pairs)  17.9 us
    all_to_all x1, starting transfers between devices, program(): blocks = lax.all_to_all(blocks, ('z', 'c'), 0, 0, tiled=True)  13 us
    ppermute x6, starting transfers between devices, shift_y(): return lax.ppermute(value, 'y', shift(4, k))  10.4 us
    pallas_call x1, Pallas kernels, main_call(): pl.pallas_call(main_kernel, out_shape=(jax.ShapeDtypeStruct((D, 1024), BF...  10 us
    all_to_all x1, waiting for transfers between devices, program(): blocks = lax.all_to_all(blocks, ('z', 'c'), 0, 0, tiled=True)  9.52 us
    ppermute x1, starting transfers between devices, program(): diag = lax.ppermute(diag, ALL, shift_both(-1))  8.18 us
    pallas_call x2, Pallas kernels, early_call(): pl.pallas_call(functools.partial(early_kernel, w), out_shape=(wide, wide,...  6.65 us
    ppermute x6, starting transfers between devices, shift_x(): return lax.ppermute(value, ('xl', 'xh'), pairs)  4.81 us
  transfers between devices with their start and end apart: 19, of which 5 were waited for; matrix products, arithmetic and copies ran while one was open for 0% of the time, Pallas kernels for 15%

profile of v2, /device:TPU:1, one launch (start us, length us, event | category | flops | bytes accessed | tf_op | source)
XLA Modules:
  0.0 103.2 jit_solution(350606184022614688)
XLA Ops:
  0.7 2.7 %pack.1 = (bf16[2,112,1024]{2,1,0:T(8,128)(2,1)}, bf16[2,112,1024]{2,1,0:T(8,128)(2,1)}, bf16[2,48,1024]{2,1,0:T(8,128)(2,1)}) custom-call(bf16[2,12,24,1024]{3,2,1,0:T(8,128)(2,1)} %x_ref.7, bf16[2,12,24,1024]{3,2,1,0:T(8,128)(2,1)} %dy_ref.7), custom_call_target="tpu_custom_call" | custom-call | flops 1000000 | bytes 4000000 | tf_op jit(solution)/shard_map/pack/pallas_call | solution.py:106
  3.4 3.3 %collective-permute-start.1 = (bf16[2,112,1024]{2,1,0:T(8,128)(2,1)}, bf16[2,112,1024]{2,1,0:T(8,128)(2,1)S(1)}, u32[]{:S(2)}, u32[]{:S(2)}) collective-permute-start(bf16[2,112,1024]{2,1,0:T(8,128)(2,1)} %get-tuple-element.55), channel_id=1, source_target_pairs={{0,31},{1,0},{2,1},{3,2},{4,3},{5,4},{6,5},{7,6},{8,7},{9,8},{10,9... | collective-permute-start | bytes 1376264 | tf_op jit(solution)/shard_map/ppermute | solution.py:642
  6.6 2.0 %collective-permute-start = (bf16[2,112,1024]{2,1,0:T(8,128)(2,1)}, bf16[2,112,1024]{2,1,0:T(8,128)(2,1)S(1)}, u32[]{:S(2)}, u32[]{:S(2)}) collective-permute-start(bf16[2,112,1024]{2,1,0:T(8,128)(2,1)} %get-tuple-element.54), channel_id=1, source_target_pairs={{0,224},{32,0},{64,32},{96,64},{128,96},{160,128},{192,160},{224,1... | collective-permute-start | bytes 1376264 | tf_op jit(solution)/shard_map/ppermute | solution.py:643
  8.6 8.2 %collective-permute-start.2 = (bf16[2,48,1024]{2,1,0:T(8,128)(2,1)}, bf16[2,48,1024]{2,1,0:T(8,128)(2,1)S(1)}, u32[]{:S(2)}, u32[]{:S(2)}) collective-permute-start(bf16[2,48,1024]{2,1,0:T(8,128)(2,1)} %get-tuple-element.58), channel_id=1, source_target_pairs={{0,255},{1,224},{2,225},{3,226},{4,227},{5,228},{6,229},{7,230},{8... | collective-permute-start | bytes 589832 | tf_op jit(solution)/shard_map/ppermute | solution.py:644
  16.8 1.9 %copy-done = bf16[1024,1536]{1,0:T(8,128)(2,1)S(1)} copy-done((bf16[1024,1536]{1,0:T(8,128)(2,1)S(1)}, bf16[1024,1536]{1,0:T(8,128)(2,1)}, u32[]{:S(2)}) %copy-start) | copy-done | bytes 3145752
  18.7 1.2 %copy-done.5 = bf16[512,1024]{1,0:T(8,128)(2,1)S(1)} copy-done((bf16[512,1024]{1,0:T(8,128)(2,1)S(1)}, bf16[512,1024]{1,0:T(8,128)(2,1)}, u32[]{:S(2)}) %copy-start.5) | copy-done | bytes 1048600
  19.9 3.3 %shard_map.84 = (bf16[144,1024]{1,0:T(8,128)(2,1)S(1)}, bf16[144,1024]{1,0:T(8,128)(2,1)S(1)}, bf16[144,1024]{1,0:T(8,128)(2,1)S(1)}, bf16[144,2048]{1,0:T(8,128)(2,1)S(1)}) custom-call(bf16[2,12,24,1024]{3,2,1,0:T(8,128)(2,1)S(1)} %copy-done.2, bf16[2,12,24,1024]{3,2,1,0:T(8,128)(2,1)S(1)} %copy-done.3, f32[1,1024]{1,0:T(1,128)S(1)} %bitcast.3, ...), custom_call_target="tpu_custom_call" | custom-call | flops 2000000000 | bytes 9000000 | tf_op jit(solution)/shard_map/pallas_call | solution.py:221
  23.2 0.0 collective-permute-done.1.refs_0_.lon_ref
  23.3 0.0 copy-start.1
  23.3 0.0 copy-start.6
  23.3 3.3 %shard_map.85 = (bf16[144,1024]{1,0:T(8,128)(2,1)S(1)}, bf16[144,1024]{1,0:T(8,128)(2,1)S(1)}, bf16[144,1024]{1,0:T(8,128)(2,1)S(1)}, bf16[144,2048]{1,0:T(8,128)(2,1)S(1)}) custom-call(bf16[2,12,24,1024]{3,2,1,0:T(8,128)(2,1)S(1)} %copy-done.2, bf16[2,12,24,1024]{3,2,1,0:T(8,128)(2,1)S(1)} %copy-done.3, ...), custom_call_target="tpu_custom_call" | custom-call | flops 2000000000 | bytes 9000000 | tf_op jit(solution)/shard_map/pallas_call | solution.py:221
  26.6 0.0 collective-permute-done.2.diag_ref
  26.6 0.0 collective-permute-done.lat_ref
  26.6 10.0 %main.1 = (bf16[1024,1024]{1,0:T(8,128)(2,1)S(1)}, bf16[1024,1024]{1,0:T(8,128)(2,1)S(1)}, bf16[576,2048]{1,0:T(8,128)(2,1)S(1)}, bf16[576,1024]{1,0:T(8,128)(2,1)S(1)}, bf16[576,1024]{1,0:T(8,128)(2,1)S(1)}) custom-call(bf16[2,12,24,1024]{3,2,1,0:T(8,128)(2,1)S(1)} %copy-done.2, bf16[2,12,24,1024]{3,2,1,0:T(8,128)(2,1)S(1)} %copy-done.3, ...), custom_call_target="tpu_custom_call" | custom-call | flops 5500000256 | bytes 14000000 | tf_op jit(solution)/shard_map/main/pallas_call | solution.py:270
  36.6 0.1 collective-permute-start.5
  36.7 2.8 %input_low.1 = (bf16[2,3,24,1024]{3,2,1,0:T(8,128)(2,1)S(1)}, bf16[112,1024]{1,0:T(8,128)(2,1)S(1)}, bf16[48,1024]{1,0:T(8,128)(2,1)S(1)}, bf16[48,1024]{1,0:T(8,128)(2,1)S(1)}, f32[1,1024]{1,0:T(1,128)S(1)}) custom-call(bf16[576,2048]{1,0:T(8,128)(2,1)S(1)} %get-tuple-element.67.gact_ref, bf16[576,1024]{1,0:T(8,128)(2,1)S(1)} %get-tuple-element.68.xw_ref, ...), custom_call_target="tpu_custom_call" | custom-call | flops 1000000000 | bytes 9000000 | tf_op jit(solution)/shard_map/input_low/pallas_call | solution.py:355
  39.5 2.8 %input_high.1 = (bf16[2,6,24,1024]{3,2,1,0:T(8,128)(2,1)S(1)}, bf16[176,1024]{1,0:T(8,128)(2,1)S(1)}, f32[8,128]{1,0:T(8,128)S(1)}) custom-call(bf16[576,2048]{1,0:T(8,128)(2,1)S(1)} %get-tuple-element.67.gact_ref, bf16[576,1024]{1,0:T(8,128)(2,1)S(1)} %get-tuple-element.68.xw_ref, bf16[576,1024]{1,0:T(8,128)(2,1)S(1)} %get-tuple-element.69.dyw_ref, ...), custom_call_target="tpu_custom_call" | custom-call | flops 1000000000 | bytes 9000000 | tf_op jit(solution)/shard_map/input_high/pallas_call | solution.py:372
  42.4 0.0 collective-permute-done.5.recv_ref
  42.4 0.5 split.1
  42.9 0.4 collective-permute-start.9
  43.3 1.7 %collective-permute-start.10 = (bf16[256,512]{1,0:T(8,128)(2,1)S(1)}, bf16[256,512]{1,0:T(8,128)(2,1)S(1)}, u32[]{:S(2)}, u32[]{:S(2)}) collective-permute-start(bf16[256,512]{1,0:T(8,128)(2,1)S(1)} %get-tuple-element.84), channel_id=1, source_target_pairs={{0,16},{16,0},{32,48},{48,32},{1,17},{17,1},{33,49},{49,33},{2,18}... | collective-permute-start | bytes 786440 | tf_op jit(solution)/shard_map/ppermute | solution.py:608
  45.0 0.3 collective-permute-start.3
  45.3 1.3 %collective-permute-start.6 = (bf16[272,512]{1,0:T(8,128)(2,1)S(1)}, bf16[272,512]{1,0:T(8,128)(2,1)S(1)}, u32[]{:S(2)}, u32[]{:S(2)}) collective-permute-start(bf16[272,512]{1,0:T(8,128)(2,1)S(1)} %get-tuple-element.79), channel_id=1, source_target_pairs={{0,64},{64,128},{128,192},{192,0},{1,65},{65,129},{129,193},{193,1... | collective-permute-start | bytes 835592 | tf_op jit(solution)/shard_map/ppermute | solution.py:612
  46.6 3.8 %collective-permute-start.7 = (bf16[272,512]{1,0:T(8,128)(2,1)S(1)}, bf16[272,512]{1,0:T(8,128)(2,1)S(1)}, u32[]{:S(2)}, u32[]{:S(2)}) collective-permute-start(bf16[272,512]{1,0:T(8,128)(2,1)S(1)} %get-tuple-element.80), channel_id=1, source_target_pairs={{0,128},{64,192},{128,0},{192,64},{1,129},{65,193},{129,1},{193,65... | collective-permute-start | bytes 835592 | tf_op jit(solution)/shard_map/ppermute | solution.py:612
  50.4 1.7 %collective-permute-done.9.b1 = bf16[256,512]{1,0:T(8,128)(2,1)S(1)} collective-permute-done((bf16[256,512]{1,0:T(8,128)(2,1)S(1)}, bf16[256,512]{1,0:T(8,128)(2,1)S(1)}, u32[]{:S(2)}, u32[]{:S(2)}) %collective-permute-start.9) | collective-permute-done | bytes 262176 | tf_op jit(solution)/shard_map/ppermute | solution.py:608
  52.2 0.0 collective-permute-start.8
  52.2 8.3 %collective-permute-done.10.b2 = bf16[256,512]{1,0:T(8,128)(2,1)S(1)} collective-permute-done((bf16[256,512]{1,0:T(8,128)(2,1)S(1)}, bf16[256,512]{1,0:T(8,128)(2,1)S(1)}, u32[]{:S(2)}, u32[]{:S(2)}) %collective-permute-start.10) | collective-permute-done | bytes 262176 | tf_op jit(solution)/shard_map/ppermute | solution.py:608
  60.4 0.0 collective-permute-start.11
  60.4 5.9 %collective-permute-done.11.b3 = bf16[256,512]{1,0:T(8,128)(2,1)S(1)} collective-permute-done((bf16[256,512]{1,0:T(8,128)(2,1)S(1)}, bf16[256,512]{1,0:T(8,128)(2,1)S(1)}, u32[]{:S(2)}, u32[]{:S(2)}) %collective-permute-start.11) | collective-permute-done | bytes 262176 | tf_op jit(solution)/shard_map/ppermute | solution.py:608
  66.3 0.0 collective-permute-done.6.a1
  66.3 0.0 collective-permute-done.7.a2
  66.3 0.0 collective-permute-done.8.a3
  66.3 0.3 cross.1
  66.6 0.1 collective-permute-start.15
  66.7 4.9 %collective-permute-start.16 = (bf16[64,512]{1,0:T(8,128)(2,1)S(1)}, bf16[64,512]{1,0:T(8,128)(2,1)S(1)}, u32[]{:S(2)}, u32[]{:S(2)}) collective-permute-start(bf16[64,512]{1,0:T(8,128)(2,1)S(1)} %get-tuple-element.95), channel_id=1, source_target_pairs={{0,128},{64,192},{128,0},{192,64},{1,129},{65,193},{129,1},{193,65... | collective-permute-start | bytes 196616 | tf_op jit(solution)/shard_map/ppermute | solution.py:612
  71.6 0.3 collective-permute-start.17
  71.9 2.7 %collective-permute-start.13 = (bf16[80,512]{1,0:T(8,128)(2,1)S(1)}, bf16[80,512]{1,0:T(8,128)(2,1)S(1)}, u32[]{:S(2)}, u32[]{:S(2)}) collective-permute-start(bf16[80,512]{1,0:T(8,128)(2,1)S(1)} %get-tuple-element.91), channel_id=1, source_target_pairs={{0,16},{16,0},{32,48},{48,32},{1,17},{17,1},{33,49},{49,33},{2,18}... | collective-permute-start | bytes 245768 | tf_op jit(solution)/shard_map/ppermute | solution.py:608
  74.6 0.0 collective-permute-done.15.b1
  74.6 0.0 collective-permute-start.14
  74.6 2.0 %collective-permute-done.12.a1 = bf16[80,512]{1,0:T(8,128)(2,1)S(1)} collective-permute-done((bf16[80,512]{1,0:T(8,128)(2,1)S(1)}, bf16[80,512]{1,0:T(8,128)(2,1)S(1)}, u32[]{:S(2)}, u32[]{:S(2)}) %collective-permute-start.12) | collective-permute-done | bytes 81952 | tf_op jit(solution)/shard_map/ppermute | solution.py:608
  76.6 0.0 collective-permute-start.4
  76.6 1.7 %join_rest.1.rest_ref = bf16[2,12,24,1024]{3,2,1,0:T(8,128)(2,1)} custom-call(bf16[2,6,24,1024]{3,2,1,0:T(8,128)(2,1)S(1)} %get-tuple-element.88.high_ref, bf16[2,3,24,1024]{3,2,1,0:T(8,128)(2,1)S(1)} %get-tuple-element.89.low_ref, bf16[176,1024]{1,0:T(8,128)(2,1)S(1)} %collective-permute-done.3.lon_ref), custom_call_target="tpu_custom_call" | custom-call | flops 1000000 | bytes 4000000 | tf_op jit(solution)/shard_map/join_rest/pallas_call | solution.py:422
  78.3 0.0 collective-permute-done.14.a3
  78.3 0.7 gather.1
  79.1 13.0 %all-to-all-start = ((bf16[16,8,640]{2,1,0:T(8,128)(2,1)}), bf16[16,8,640]{2,1,0:T(8,128)(2,1)S(1)}, u32[]{:S(2)}, u32[]{:S(2)}) async-start(bf16[16,8,640]{2,1,0:T(8,128)(2,1)} %gather.1), calls=%async_computation | async-start | bytes 327680 | tf_op jit(solution)/shard_map/all_to_all | solution.py:664
  92.1 9.5 %all-to-all-done.blocks = bf16[16,8,640]{2,1,0:T(8,128)(2,1)S(1)} async-done(((bf16[16,8,640]{2,1,0:T(8,128)(2,1)}), bf16[16,8,640]{2,1,0:T(8,128)(2,1)S(1)}, u32[]{:S(2)}, u32[]{:S(2)}) %all-to-all-start) | async-done | bytes 163872 | tf_op jit(solution)/shard_map/all_to_all | solution.py:664
  101.7 0.6 final.1
  102.3 0.9 join_top.1
  (18 shorter events, 0.1 us)
Async XLA Ops:
  0.6 16.1 %copy-start.3 = (bf16[2,12,24,1024]{3,2,1,0:T(8,128)(2,1)S(1)}, bf16[2,12,24,1024]{3,2,1,0:T(8,128)(2,1)}, u32[]{:S(2)}) copy-start(bf16[2,12,24,1024]{3,2,1,0:T(8,128)(2,1)} %dy_ref.7) | copy-start | bytes 3538948
  0.6 16.1 %copy-start.2 = (bf16[2,12,24,1024]{3,2,1,0:T(8,128)(2,1)S(1)}, bf16[2,12,24,1024]{3,2,1,0:T(8,128)(2,1)}, u32[]{:S(2)}) copy-start(bf16[2,12,24,1024]{3,2,1,0:T(8,128)(2,1)} %x_ref.7) | copy-start | bytes 3538948
  0.7 16.1 %copy-start.4 = (f32[1024]{0:T(1024)S(1)}, f32[1024]{0:T(1024)}, u32[]{:S(2)}) copy-start(f32[1024]{0:T(1024)} %param.7) | copy-start | bytes 12292
  3.4 19.9 %collective-permute-start.1 = (bf16[2,112,1024]{2,1,0:T(8,128)(2,1)}, bf16[2,112,1024]{2,1,0:T(8,128)(2,1)S(1)}, u32[]{:S(2)}, u32[]{:S(2)}) collective-permute-start(bf16[2,112,1024]{2,1,0:T(8,128)(2,1)} %get-tuple-element.55), channel_id=1, source_target_pairs={{0,31},{1,0},{2,1},{3,2},{4,3},{5,4},{6,5},{7,6},{8,7},{9,8},{10,9... | collective-permute-start | bytes 1376264 | tf_op jit(solution)/shard_map/ppermute | solution.py:642
  6.6 20.0 %collective-permute-start = (bf16[2,112,1024]{2,1,0:T(8,128)(2,1)}, bf16[2,112,1024]{2,1,0:T(8,128)(2,1)S(1)}, u32[]{:S(2)}, u32[]{:S(2)}) collective-permute-start(bf16[2,112,1024]{2,1,0:T(8,128)(2,1)} %get-tuple-element.54), channel_id=1, source_target_pairs={{0,224},{32,0},{64,32},{96,64},{128,96},{160,128},{192,160},{224,1... | collective-permute-start | bytes 1376264 | tf_op jit(solution)/shard_map/ppermute | solution.py:643
  8.6 18.0 %collective-permute-start.2 = (bf16[2,48,1024]{2,1,0:T(8,128)(2,1)}, bf16[2,48,1024]{2,1,0:T(8,128)(2,1)S(1)}, u32[]{:S(2)}, u32[]{:S(2)}) collective-permute-start(bf16[2,48,1024]{2,1,0:T(8,128)(2,1)} %get-tuple-element.58), channel_id=1, source_target_pairs={{0,255},{1,224},{2,225},{3,226},{4,227},{5,228},{6,229},{7,230},{8... | collective-permute-start | bytes 589832 | tf_op jit(solution)/shard_map/ppermute | solution.py:644
  16.8 1.9 %copy-start = (bf16[1024,1536]{1,0:T(8,128)(2,1)S(1)}, bf16[1024,1536]{1,0:T(8,128)(2,1)}, u32[]{:S(2)}) copy-start(bf16[1024,1536]{1,0:T(8,128)(2,1)} %wq_ref.5) | copy-start | bytes 9437188
  18.7 1.2 %copy-start.5 = (bf16[512,1024]{1,0:T(8,128)(2,1)S(1)}, bf16[512,1024]{1,0:T(8,128)(2,1)}, u32[]{:S(2)}) copy-start(bf16[512,1024]{1,0:T(8,128)(2,1)} %wp_ref.1) | copy-start | bytes 3145732
  23.3 3.4 %copy-start.1 = (bf16[1024,1536]{1,0:T(8,128)(2,1)S(1)}, bf16[1024,1536]{1,0:T(8,128)(2,1)}, u32[]{:S(2)}) copy-start(bf16[1024,1536]{1,0:T(8,128)(2,1)} %wq_ref.5) | copy-start | bytes 9437188
  23.3 3.4 %copy-start.6 = (bf16[512,1024]{1,0:T(8,128)(2,1)S(1)}, bf16[512,1024]{1,0:T(8,128)(2,1)}, u32[]{:S(2)}) copy-start(bf16[512,1024]{1,0:T(8,128)(2,1)} %wp_ref.1) | copy-start | bytes 3145732
  36.6 5.7 %collective-permute-start.5 = (bf16[1024,1024]{1,0:T(8,128)(2,1)S(1)}, bf16[1024,1024]{1,0:T(8,128)(2,1)S(1)}, u32[]{:S(2)}, u32[]{:S(2)}) collective-permute-start(bf16[1024,1024]{1,0:T(8,128)(2,1)S(1)} %get-tuple-element.76), channel_id=1, source_target_pairs={{0,1},{1,0},{2,3},{3,2},{4,5},{5,4},{6,7},{7,6},{8,9},{9,8},{10,11... | collective-permute-start | bytes 6291464 | tf_op jit(solution)/shard_map/ppermute | solution.py:649
  42.9 9.3 %collective-permute-start.9 = (bf16[256,512]{1,0:T(8,128)(2,1)S(1)}, bf16[256,512]{1,0:T(8,128)(2,1)S(1)}, u32[]{:S(2)}, u32[]{:S(2)}) collective-permute-start(bf16[256,512]{1,0:T(8,128)(2,1)S(1)} %get-tuple-element.83), channel_id=1, source_target_pairs={{0,32},{16,48},{32,16},{48,0},{1,33},{17,49},{33,17},{49,1},{2,34}... | collective-permute-start | bytes 786440 | tf_op jit(solution)/shard_map/ppermute | solution.py:608
  43.3 17.2 %collective-permute-start.10 = (bf16[256,512]{1,0:T(8,128)(2,1)S(1)}, bf16[256,512]{1,0:T(8,128)(2,1)S(1)}, u32[]{:S(2)}, u32[]{:S(2)}) collective-permute-start(bf16[256,512]{1,0:T(8,128)(2,1)S(1)} %get-tuple-element.84), channel_id=1, source_target_pairs={{0,16},{16,0},{32,48},{48,32},{1,17},{17,1},{33,49},{49,33},{2,18}... | collective-permute-start | bytes 786440 | tf_op jit(solution)/shard_map/ppermute | solution.py:608
  45.0 21.7 %collective-permute-start.3 = (bf16[176,1024]{1,0:T(8,128)(2,1)S(1)}, bf16[176,1024]{1,0:T(8,128)(2,1)S(1)}, u32[]{:S(2)}, u32[]{:S(2)}) collective-permute-start(bf16[176,1024]{1,0:T(8,128)(2,1)S(1)} %get-tuple-element.74), channel_id=1, source_target_pairs={{0,1},{1,2},{2,3},{3,4},{4,5},{5,6},{6,7},{7,8},{8,9},{9,10},{10,1... | collective-permute-start | bytes 1081352 | tf_op jit(solution)/shard_map/ppermute | solution.py:655
  45.3 21.1 %collective-permute-start.6 = (bf16[272,512]{1,0:T(8,128)(2,1)S(1)}, bf16[272,512]{1,0:T(8,128)(2,1)S(1)}, u32[]{:S(2)}, u32[]{:S(2)}) collective-permute-start(bf16[272,512]{1,0:T(8,128)(2,1)S(1)} %get-tuple-element.79), channel_id=1, source_target_pairs={{0,64},{64,128},{128,192},{192,0},{1,65},{65,129},{129,193},{193,1... | collective-permute-start | bytes 835592 | tf_op jit(solution)/shard_map/ppermute | solution.py:612
  46.6 19.8 %collective-permute-start.7 = (bf16[272,512]{1,0:T(8,128)(2,1)S(1)}, bf16[272,512]{1,0:T(8,128)(2,1)S(1)}, u32[]{:S(2)}, u32[]{:S(2)}) collective-permute-start(bf16[272,512]{1,0:T(8,128)(2,1)S(1)} %get-tuple-element.80), channel_id=1, source_target_pairs={{0,128},{64,192},{128,0},{192,64},{1,129},{65,193},{129,1},{193,65... | collective-permute-start | bytes 835592 | tf_op jit(solution)/shard_map/ppermute | solution.py:612
  52.2 14.2 %collective-permute-start.8 = (bf16[272,512]{1,0:T(8,128)(2,1)S(1)}, bf16[272,512]{1,0:T(8,128)(2,1)S(1)}, u32[]{:S(2)}, u32[]{:S(2)}) collective-permute-start(bf16[272,512]{1,0:T(8,128)(2,1)S(1)} %get-tuple-element.81), channel_id=1, source_target_pairs={{0,192},{64,0},{128,64},{192,128},{1,193},{65,1},{129,65},{193,129... | collective-permute-start | bytes 835592 | tf_op jit(solution)/shard_map/ppermute | solution.py:612
  60.4 5.9 %collective-permute-start.11 = (bf16[256,512]{1,0:T(8,128)(2,1)S(1)}, bf16[256,512]{1,0:T(8,128)(2,1)S(1)}, u32[]{:S(2)}, u32[]{:S(2)}) collective-permute-start(bf16[256,512]{1,0:T(8,128)(2,1)S(1)} %get-tuple-element.85), channel_id=1, source_target_pairs={{0,48},{16,32},{32,0},{48,16},{1,49},{17,33},{33,1},{49,17},{2,50}... | collective-permute-start | bytes 786440 | tf_op jit(solution)/shard_map/ppermute | solution.py:608
  66.6 8.0 %collective-permute-start.15 = (bf16[64,512]{1,0:T(8,128)(2,1)S(1)}, bf16[64,512]{1,0:T(8,128)(2,1)S(1)}, u32[]{:S(2)}, u32[]{:S(2)}) collective-permute-start(bf16[64,512]{1,0:T(8,128)(2,1)S(1)} %get-tuple-element.94), channel_id=1, source_target_pairs={{0,64},{64,128},{128,192},{192,0},{1,65},{65,129},{129,193},{193,1... | collective-permute-start | bytes 196616 | tf_op jit(solution)/shard_map/ppermute | solution.py:612
  66.7 11.6 %collective-permute-start.16 = (bf16[64,512]{1,0:T(8,128)(2,1)S(1)}, bf16[64,512]{1,0:T(8,128)(2,1)S(1)}, u32[]{:S(2)}, u32[]{:S(2)}) collective-permute-start(bf16[64,512]{1,0:T(8,128)(2,1)S(1)} %get-tuple-element.95), channel_id=1, source_target_pairs={{0,128},{64,192},{128,0},{192,64},{1,129},{65,193},{129,1},{193,65... | collective-permute-start | bytes 196616 | tf_op jit(solution)/shard_map/ppermute | solution.py:612
  71.6 6.7 %collective-permute-start.17 = (bf16[64,512]{1,0:T(8,128)(2,1)S(1)}, bf16[64,512]{1,0:T(8,128)(2,1)S(1)}, u32[]{:S(2)}, u32[]{:S(2)}) collective-permute-start(bf16[64,512]{1,0:T(8,128)(2,1)S(1)} %get-tuple-element.96), channel_id=1, source_target_pairs={{0,192},{64,0},{128,64},{192,128},{1,193},{65,1},{129,65},{193,129... | collective-permute-start | bytes 196616 | tf_op jit(solution)/shard_map/ppermute | solution.py:612
  71.9 4.7 %collective-permute-start.12 = (bf16[80,512]{1,0:T(8,128)(2,1)S(1)}, bf16[80,512]{1,0:T(8,128)(2,1)S(1)}, u32[]{:S(2)}, u32[]{:S(2)}) collective-permute-start(bf16[80,512]{1,0:T(8,128)(2,1)S(1)} %get-tuple-element.87), channel_id=1, source_target_pairs={{0,32},{16,48},{32,16},{48,0},{1,33},{17,49},{33,17},{49,1},{2,34}... | collective-permute-start | bytes 245768 | tf_op jit(solution)/shard_map/ppermute | solution.py:608
  71.9 6.4 %collective-permute-start.13 = (bf16[80,512]{1,0:T(8,128)(2,1)S(1)}, bf16[80,512]{1,0:T(8,128)(2,1)S(1)}, u32[]{:S(2)}, u32[]{:S(2)}) collective-permute-start(bf16[80,512]{1,0:T(8,128)(2,1)S(1)} %get-tuple-element.91), channel_id=1, source_target_pairs={{0,16},{16,0},{32,48},{48,32},{1,17},{17,1},{33,49},{49,33},{2,18}... | collective-permute-start | bytes 245768 | tf_op jit(solution)/shard_map/ppermute | solution.py:608
  74.6 3.7 %collective-permute-start.14 = (bf16[80,512]{1,0:T(8,128)(2,1)S(1)}, bf16[80,512]{1,0:T(8,128)(2,1)S(1)}, u32[]{:S(2)}, u32[]{:S(2)}) collective-permute-start(bf16[80,512]{1,0:T(8,128)(2,1)S(1)} %get-tuple-element.92), channel_id=1, source_target_pairs={{0,48},{16,32},{32,0},{48,16},{1,49},{17,33},{33,1},{49,17},{2,50}... | collective-permute-start | bytes 245768 | tf_op jit(solution)/shard_map/ppermute | solution.py:608
  76.6 15.5 %collective-permute-start.4 = (bf16[160,1024]{1,0:T(8,128)(2,1)S(1)}, bf16[160,1024]{1,0:T(8,128)(2,1)S(1)}, u32[]{:S(2)}, u32[]{:S(2)}) collective-permute-start(bf16[160,1024]{1,0:T(8,128)(2,1)S(1)} %pad_maximum_fusion), channel_id=1, source_target_pairs={{0,32},{32,64},{64,96},{96,128},{128,160},{160,192},{192,224},{224... | collective-permute-start | bytes 983048 | tf_op jit(solution)/shard_map/ppermute | solution.py:660
  79.1 22.6 %all-to-all-start = ((bf16[16,8,640]{2,1,0:T(8,128)(2,1)}), bf16[16,8,640]{2,1,0:T(8,128)(2,1)S(1)}, u32[]{:S(2)}, u32[]{:S(2)}) async-start(bf16[16,8,640]{2,1,0:T(8,128)(2,1)} %gather.1), calls=%async_computation | async-start | bytes 327680 | tf_op jit(solution)/shard_map/all_to_all | solution.py:664
